TPU v7x, 32 devices: a whole 2x2x4 slice. The times are simulated.
32 devices in a mesh: tp: 2 (over x), sp: 16 (over z, y, core).
Axes of the slice: x: 2, y: 2, z: 4, core: 2. Of those that a mesh axis runs over, the one named last changes fastest.
Arguments:
- tokens: bfloat16 [2048, 2048], P('sp'), may hold values from -6 to 6
- item_lengths: int32 [4], replicated, may hold values from 128 to 1536, as said below
- first_gain: bfloat16 [2048], replicated, may hold values from 0.25 to 1.75
- query_weight: bfloat16 [2048, 2048], P('tp'), may hold values from -0.125 to 0.125
- key_weight: bfloat16 [1024, 2048], P('tp'), may hold values from -0.125 to 0.125
- value_weight: bfloat16 [1024, 2048], P('tp'), may hold values from -0.125 to 0.125
- headgate_weight: bfloat16 [16, 2048], P('tp'), may hold values from -0.125 to 0.125
- merge_weight: bfloat16 [2048, 2048], P(None, 'tp'), may hold values from -1 to 1
- query_norm: bfloat16 [128], replicated, may hold values from 0.8984375 to 2
- key_norm: bfloat16 [128], replicated, may hold values from 0.8984375 to 2
- second_gain: bfloat16 [2048], replicated, may hold values from 0.25 to 1.75
- gate_weight: bfloat16 [6144, 2048], P(('tp', 'sp')), may hold values from -0.125 to 0.125
- up_weight: bfloat16 [6144, 2048], P(('tp', 'sp')), may hold values from -0.125 to 0.125
- down_weight: bfloat16 [6144, 2048], P(('tp', 'sp')), may hold values from -0.078125 to 0.078125
- out_cotangent: bfloat16 [2048, 2048], P('sp')
Outputs:
- layer_output: bfloat16 [2048, 2048], P('sp')
- input_grad: float32 [2048, 2048], P('sp')
- first_grad: float32 [2048], replicated
- query_grad: float32 [2048, 2048], P('tp')
- key_grad: float32 [1024, 2048], P('tp')
- value_grad: float32 [1024, 2048], P('tp')
- headgate_grad: float32 [16, 2048], P('tp')
- merge_grad: float32 [2048, 2048], P(None, 'tp')
- query_norm_grad: float32 [128], replicated
- key_norm_grad: float32 [128], replicated
- second_grad: float32 [2048], replicated
- gate_grad: float32 [6144, 2048], P(('tp', 'sp'))
- up_grad: float32 [6144, 2048], P(('tp', 'sp'))
- down_grad: float32 [6144, 2048], P(('tp', 'sp'))
Inputs may be any that keep to these rules, and one draw needn't show every extreme that they name: `item_lengths`: the item lengths sum to 2048; exactly one item has 1536 tokens, every other at least 128.
All inputs are finite; a program needn't handle non-finite values.
Results may differ from a plain program's by a relative error of at most 0.02.
Values may be sent and summed in bfloat16 or wider, within the bound.
No kernel may reach another device: no remote copies, remote signals or barrier semaphores. Data moves between devices by JAX's collectives and lax.ppermute only.
A program may use at most 384 MiB of HBM per device.

v0:
```python
import math

import jax
import jax.numpy as jnp
from jax import lax
from jax.sharding import PartitionSpec as P

EPS = 1e-06
THETA = 1000000.0
NEG = -1e30


def right_dot(first_matrix, second_matrix):
    return lax.dot_general(
        first_matrix, second_matrix, (((1,), (1,)), ((), ())), preferred_element_type=jnp.float32
    )


def plain_dot(first_matrix, second_matrix):
    return jnp.dot(first_matrix, second_matrix, preferred_element_type=jnp.float32)


def outer_dot(first_matrix, second_matrix):
    return lax.dot_general(
        first_matrix, second_matrix, (((0,), (0,)), ((), ())), preferred_element_type=jnp.float32
    )


def normalize(values, gain_vector):
    inverse = lax.rsqrt(jnp.mean(values * values, axis=-1, keepdims=True) + EPS)
    return (values * inverse * gain_vector, inverse)


def normalize_back(values, inverse, gain_vector, upstream):
    weighted = upstream * gain_vector
    inner_mean = jnp.mean(weighted * values, axis=-1, keepdims=True)
    return (
        inverse * weighted - values * inverse * inverse * inverse * inner_mean,
        values * inverse * upstream,
    )


def rotary_tables(positions, head_width):
    half_width = head_width // 2
    frequency = THETA ** (-2.0 * jnp.arange(half_width, dtype=jnp.float32) / head_width)
    angles = positions.astype(jnp.float32)[:, None] * frequency[None, :]
    return (jnp.cos(angles)[:, None, :], jnp.sin(angles)[:, None, :])


def rotate(values, cosine_table, sine_table):
    half_width = values.shape[-1] // 2
    former = values[..., :half_width]
    latter = values[..., half_width:]
    return jnp.concatenate(
        [former * cosine_table - latter * sine_table, latter * cosine_table + former * sine_table],
        axis=-1,
    )


def item_geometry(item_lengths, first_row, row_count):
    item_ends = jnp.cumsum(item_lengths)
    item_starts = item_ends - item_lengths
    row_index = first_row + jnp.arange(row_count, dtype=jnp.int32)
    begins = jnp.max(
        jnp.where(item_starts[None, :] <= row_index[:, None], item_starts[None, :], 0), axis=1
    )
    return (row_index, begins)


def block_scores(queries, key_block, block_start, row_index, begins, score_scale):
    scores = (
        jnp.einsum("rkgd,skd->kgrs", queries, key_block, preferred_element_type=jnp.float32)
        * score_scale
    )
    key_index = block_start + jnp.arange(key_block.shape[0], dtype=jnp.int32)
    valid = (key_index[None, :] >= begins[:, None]) & (key_index[None, :] <= row_index[:, None])
    return (jnp.where(valid, scores, NEG), valid)


def swiglu(inputs_low, gate_rows, up_rows):
    gate_pre = right_dot(inputs_low, gate_rows)
    up_pre = right_dot(inputs_low, up_rows)
    return (gate_pre, up_pre, (jax.nn.silu(gate_pre) * up_pre).astype(jnp.bfloat16))


def swiglu_back(gate_pre, up_pre, grad_act):
    sigma = jax.nn.sigmoid(gate_pre)
    grad_gate = grad_act * up_pre * sigma * (1.0 + gate_pre * (1.0 - sigma))
    grad_up = grad_act * gate_pre * sigma
    return (grad_gate.astype(jnp.bfloat16), grad_up.astype(jnp.bfloat16))


def shards(
    tokens,
    item_lengths,
    first_gain,
    query_weight,
    key_weight,
    value_weight,
    headgate_weight,
    merge_weight,
    query_norm,
    key_norm,
    second_gain,
    gate_weight,
    up_weight,
    down_weight,
    out_cotangent,
):
    sp_size = lax.axis_size("sp")
    local_rows = tokens.shape[0]
    total_rows = local_rows * sp_size
    head_width = query_norm.shape[0]
    local_heads = query_weight.shape[0] // head_width
    local_groups = key_weight.shape[0] // head_width
    group_size = local_heads // local_groups
    score_scale = 1.0 / math.sqrt(head_width)
    first_row = lax.axis_index("sp") * local_rows
    row_index, begins = item_geometry(item_lengths, first_row, local_rows)
    cosine_table, sine_table = rotary_tables(row_index - begins, head_width)
    last_row = first_row + local_rows - 1
    first_begin = begins[0]
    residual = tokens.astype(jnp.float32)
    first_gain_f = first_gain.astype(jnp.float32)
    second_gain_f = second_gain.astype(jnp.float32)
    query_gain = query_norm.astype(jnp.float32)
    key_gain = key_norm.astype(jnp.float32)
    normed, first_inverse = normalize(residual, first_gain_f)
    normed_low = normed.astype(jnp.bfloat16)
    query_heads = right_dot(normed_low, query_weight).reshape(local_rows, local_heads, head_width)
    key_heads = right_dot(normed_low, key_weight).reshape(local_rows, local_groups, head_width)
    value_low = right_dot(normed_low, value_weight).astype(jnp.bfloat16)
    gate_logit = right_dot(normed_low, headgate_weight)
    query_unit, query_inverse = normalize(query_heads, query_gain)
    key_unit, key_inverse = normalize(key_heads, key_gain)
    queries = (
        rotate(query_unit, cosine_table, sine_table)
        .astype(jnp.bfloat16)
        .reshape(local_rows, local_groups, group_size, head_width)
    )
    keys_low = (
        rotate(key_unit, cosine_table, sine_table)
        .astype(jnp.bfloat16)
        .reshape(local_rows, local_groups * head_width)
    )
    keys_all, values_all = (
        lax.all_gather(keys_low, "sp", axis=0, tiled=True),
        lax.all_gather(value_low, "sp", axis=0, tiled=True),
    )
    block_size = math.gcd(total_rows, 1024)
    block_count = total_rows // block_size
    key_blocks = keys_all.reshape(block_count, block_size, local_groups, head_width)
    value_blocks = values_all.reshape(block_count, block_size, local_groups, head_width)
    block_starts = jnp.arange(block_count, dtype=jnp.int32) * block_size

    def needed(block_start):
        return (block_start <= last_row) & (block_start + block_size > first_begin)

    def first_pass(carried, inputs):
        key_block, value_block, block_start = inputs

        def first_update(current):
            running_max, running_sum = current
            scores, valid = block_scores(
                queries, key_block, block_start, row_index, begins, score_scale
            )
            new_max = jnp.maximum(running_max, jnp.max(scores, axis=-1))
            weights = jnp.where(valid, jnp.exp(scores - new_max[..., None]), 0.0)
            return (
                new_max,
                running_sum * jnp.exp(running_max - new_max) + jnp.sum(weights, axis=-1),
            )

        def first_unchanged(current):
            return current

        return (lax.cond(needed(block_start), first_update, first_unchanged, carried), None)

    start_max = jnp.full((local_groups, group_size, local_rows), NEG, jnp.float32)
    start_sum = jnp.zeros((local_groups, group_size, local_rows), jnp.float32)
    (running_max, running_sum), _ = lax.scan(
        first_pass, (start_max, start_sum), (key_blocks, value_blocks, block_starts)
    )
    log_total = running_max + jnp.log(running_sum)

    def second_pass(carried, inputs):
        key_block, value_block, block_start = inputs

        def second_update(current):
            scores, valid = block_scores(
                queries, key_block, block_start, row_index, begins, score_scale
            )
            probs = jnp.where(valid, jnp.exp(scores - log_total[..., None]), 0.0).astype(
                jnp.bfloat16
            )
            return current + jnp.einsum(
                "kgrs,skd->kgrd", probs, value_block, preferred_element_type=jnp.float32
            )

        def second_unchanged(current):
            return current

        return (lax.cond(needed(block_start), second_update, second_unchanged, carried), None)

    start_acc = jnp.zeros((local_groups, group_size, local_rows, head_width), jnp.float32)
    accumulated, _ = lax.scan(second_pass, start_acc, (key_blocks, value_blocks, block_starts))
    attended = jnp.transpose(accumulated, (2, 0, 1, 3)).reshape(local_rows, local_heads, head_width)
    gate_value = jax.nn.sigmoid(gate_logit)
    gated_low = (
        (attended * gate_value[..., None])
        .astype(jnp.bfloat16)
        .reshape(local_rows, local_heads * head_width)
    )
    attention_out = lax.psum(right_dot(gated_low, merge_weight).astype(jnp.bfloat16), "tp").astype(
        jnp.float32
    )
    hidden = residual + attention_out
    normed_second, second_inverse = normalize(hidden, second_gain_f)
    second_low = normed_second.astype(jnp.bfloat16)
    acts_all = swiglu(lax.all_gather(second_low, "sp", axis=0, tiled=True), gate_weight, up_weight)[
        2
    ]
    branch_part = lax.psum_scatter(
        plain_dot(acts_all, down_weight), "sp", scatter_dimension=0, tiled=True
    )
    branch_out = lax.psum(branch_part.astype(jnp.bfloat16), "tp").astype(jnp.float32)
    layer_output = (hidden + branch_out).astype(jnp.bfloat16)
    grad_out = out_cotangent.astype(jnp.float32)
    stacked_weights = jnp.concatenate([gate_weight, up_weight], axis=0)
    inputs_low = lax.all_gather(second_low, "sp", axis=0, tiled=True)
    grads_low = lax.all_gather(out_cotangent, "sp", axis=0, tiled=True)
    gate_pre, up_pre, act_low = swiglu(inputs_low, gate_weight, up_weight)
    grad_act = right_dot(grads_low, down_weight)
    grad_gate, grad_up = swiglu_back(gate_pre, up_pre, grad_act)
    gate_acc = outer_dot(grad_gate, inputs_low)
    up_acc = outer_dot(grad_up, inputs_low)
    down_acc = outer_dot(act_low, grads_low)
    fold_stacked_grads = jnp.concatenate([grad_gate, grad_up], axis=1)
    second_part = lax.psum_scatter(
        plain_dot(fold_stacked_grads, stacked_weights), "sp", scatter_dimension=0, tiled=True
    )
    grad_second = lax.psum(second_part.astype(jnp.bfloat16), "tp").astype(jnp.float32)
    grad_hidden_norm, second_terms = normalize_back(
        hidden, second_inverse, second_gain_f, grad_second
    )
    hidden_grad = grad_out + grad_hidden_norm
    hidden_low = hidden_grad.astype(jnp.bfloat16)
    merge_grad = outer_dot(hidden_low, gated_low)
    grad_gated = plain_dot(hidden_low, merge_weight).reshape(local_rows, local_heads, head_width)
    grad_attended_low = (grad_gated * gate_value[..., None]).astype(jnp.bfloat16)
    grad_logit_low = (
        jnp.sum(grad_gated * attended, axis=-1) * gate_value * (1.0 - gate_value)
    ).astype(jnp.bfloat16)
    row_delta = jnp.sum(grad_attended_low.astype(jnp.float32) * attended, axis=-1).reshape(
        local_rows, local_groups, group_size
    )
    row_delta = jnp.transpose(row_delta, (1, 2, 0))
    grad_grouped = grad_attended_low.reshape(local_rows, local_groups, group_size, head_width)

    def back_pass(carried, inputs):
        key_block, value_block, block_start = inputs

        def back_update(grad_queries):
            scores, valid = block_scores(
                queries, key_block, block_start, row_index, begins, score_scale
            )
            probs = jnp.where(valid, jnp.exp(scores - log_total[..., None]), 0.0)
            grad_probs = jnp.einsum(
                "rkgd,skd->kgrs", grad_grouped, value_block, preferred_element_type=jnp.float32
            )
            grad_scores = (probs * (grad_probs - row_delta[..., None])).astype(jnp.bfloat16)
            grad_queries = (
                grad_queries
                + jnp.einsum(
                    "kgrs,skd->rkgd", grad_scores, key_block, preferred_element_type=jnp.float32
                )
                * score_scale
            )
            grad_keys = (
                jnp.einsum(
                    "kgrs,rkgd->skd", grad_scores, queries, preferred_element_type=jnp.float32
                )
                * score_scale
            )
            grad_values = jnp.einsum(
                "kgrs,rkgd->skd",
                probs.astype(jnp.bfloat16),
                grad_grouped,
                preferred_element_type=jnp.float32,
            )
            return (grad_queries, (grad_keys, grad_values))

        def skipped(grad_queries):
            empty = jnp.zeros((block_size, local_groups, head_width), jnp.float32)
            return (grad_queries, (empty, empty))

        return lax.cond(needed(block_start), back_update, skipped, carried)

    start_queries = jnp.zeros((local_rows, local_groups, group_size, head_width), jnp.float32)
    grad_queries, (key_parts, value_parts) = lax.scan(
        back_pass, start_queries, (key_blocks, value_blocks, block_starts)
    )
    key_terms = key_parts.reshape(total_rows, local_groups * head_width)
    value_terms = value_parts.reshape(total_rows, local_groups * head_width)
    key_sum, value_sum = (
        lax.psum_scatter(key_terms, "sp", scatter_dimension=0, tiled=True),
        lax.psum_scatter(value_terms, "sp", scatter_dimension=0, tiled=True),
    )
    grad_query_unit = rotate(
        grad_queries.reshape(local_rows, local_heads, head_width), cosine_table, -sine_table
    )
    grad_query_raw, query_gain_terms = normalize_back(
        query_heads, query_inverse, query_gain, grad_query_unit
    )
    grad_key_unit = rotate(
        key_sum.reshape(local_rows, local_groups, head_width), cosine_table, -sine_table
    )
    grad_key_raw, key_gain_terms = normalize_back(key_heads, key_inverse, key_gain, grad_key_unit)
    query_low = grad_query_raw.reshape(local_rows, local_heads * head_width).astype(jnp.bfloat16)
    key_low = grad_key_raw.reshape(local_rows, local_groups * head_width).astype(jnp.bfloat16)
    value_grad_low = value_sum.astype(jnp.bfloat16)
    query_grad = outer_dot(query_low, normed_low)
    key_grad = outer_dot(key_low, normed_low)
    value_grad = outer_dot(value_grad_low, normed_low)
    headgate_grad = outer_dot(grad_logit_low, normed_low)
    input_part = (
        plain_dot(query_low, query_weight)
        + plain_dot(key_low, key_weight)
        + plain_dot(value_grad_low, value_weight)
        + plain_dot(grad_logit_low, headgate_weight)
    )
    input_sum, query_gain_sum, key_gain_sum = (
        lax.psum(input_part.astype(jnp.bfloat16), "tp").astype(jnp.float32),
        lax.psum(jnp.sum(query_gain_terms, axis=(0, 1)).astype(jnp.bfloat16), "tp").astype(
            jnp.float32
        ),
        lax.psum(jnp.sum(key_gain_terms, axis=(0, 1)).astype(jnp.bfloat16), "tp").astype(
            jnp.float32
        ),
    )
    grad_residual_norm, first_terms = normalize_back(
        residual, first_inverse, first_gain_f, input_sum
    )
    input_grad = hidden_grad + grad_residual_norm
    reduced = lax.psum(
        (
            query_grad,
            key_grad,
            value_grad,
            headgate_grad,
            merge_grad,
            query_gain_sum,
            key_gain_sum,
            jnp.sum(first_terms, axis=0),
            jnp.sum(second_terms, axis=0),
        ),
        "sp",
    )
    return (
        layer_output,
        input_grad,
        reduced[7],
        reduced[0],
        reduced[1],
        reduced[2],
        reduced[3],
        reduced[4],
        reduced[5],
        reduced[6],
        reduced[8],
        gate_acc,
        up_acc,
        down_acc,
    )


def solution(mesh):
    return jax.shard_map(
        shards,
        mesh=mesh,
        in_specs=(
            P("sp", None),
            P(),
            P(),
            P("tp", None),
            P("tp", None),
            P("tp", None),
            P("tp", None),
            P(None, "tp"),
            P(),
            P(),
            P(),
            P(("tp", "sp"), None),
            P(("tp", "sp"), None),
            P(("tp", "sp"), None),
            P("sp", None),
        ),
        out_specs=(
            P("sp", None),
            P("sp", None),
            P(),
            P("tp", None),
            P("tp", None),
            P("tp", None),
            P("tp", None),
            P(None, "tp"),
            P(),
            P(),
            P(),
            P(("tp", "sp"), None),
            P(("tp", "sp"), None),
            P(("tp", "sp"), None),
        ),
        check_vma=False,
    )
```

profile of v0, /device:TPU:17, one launch (start us, length us, event | category | flops | bytes accessed | tf_op | source)
XLA Modules:
  0.0 1401.6 jit_solution(12109485041984418641)
XLA Ops:
  24.9 29.0 %all-gather.7.cloned.1.call-done = bf16[2048,512]{1,0:T(8,128)(2,1)} async-done(((bf16[128,512]{1,0:T(8,128)(2,1)}), bf16[2048,512]{1,0:T(8,128)(2,1)}) %all-gather.7.cloned.1.call-update) | async-done | bytes 2097168 | tf_op jit(solution)/shard_map/all_gather | solution.py:148
  61.0 35.8 %all-gather.5.cloned.1.call-done = bf16[2048,512]{1,0:T(8,128)(2,1)} async-done(((bf16[128,512]{1,0:T(8,128)(2,1)}), bf16[2048,512]{1,0:T(8,128)(2,1)}) %all-gather.5.cloned.1.call-update) | async-done | bytes 2097168 | tf_op jit(solution)/shard_map/all_gather | solution.py:147
  104.0 11.8 while.45
  115.8 12.8 while.46
  137.2 27.7 %all-reduce.9.cloned.1.call-done = bf16[128,2048]{1,0:T(8,128)(2,1)} async-done(((bf16[128,2048]{1,0:T(8,128)(2,1)}), bf16[128,2048]{1,0:T(8,128)(2,1)}) %all-reduce.9.cloned.1.call-update) | async-done | bytes 524304 | tf_op jit(solution)/shard_map/psum | solution.py:214
  168.3 73.3 %all-gather.11.cloned.1.call-done = bf16[2048,2048]{1,0:T(8,128)(2,1)} async-done(((bf16[128,2048]{1,0:T(8,128)(2,1)}), bf16[2048,2048]{1,0:T(8,128)(2,1)}) %all-gather.11.cloned.1.call-update) | async-done | bytes 8388624 | tf_op jit(solution)/shard_map/all_gather | solution.py:231
  241.7 7.6 fusion.129
  249.3 68.4 %all-gather.9.cloned.1.call-done = bf16[2048,2048]{1,0:T(8,128)(2,1)} async-done(((bf16[128,2048]{1,0:T(8,128)(2,1)}), bf16[2048,2048]{1,0:T(8,128)(2,1)}) %all-gather.9.cloned.1.call-update) | async-done | bytes 8388624 | tf_op jit(solution)/shard_map/all_gather | solution.py:220
  329.8 8.2 fusion.61
  338.1 176.3 %reduce-scatter.7.cloned.1.call-done = f32[128,2048]{1,0:T(8,128)} async-done(((f32[2048,2048]{1,0:T(8,128)}), f32[128,2048]{1,0:T(8,128)}) %reduce-scatter.7.cloned.1.call-update) | async-done | bytes 1048592 | tf_op jit(solution)/shard_map/reduce_scatter | solution.py:239
  516.5 9.6 fusion.128
  526.3 19.7 %all-reduce.11.cloned.1.call-done = bf16[128,2048]{1,0:T(8,128)(2,1)} async-done(((bf16[128,2048]{1,0:T(8,128)(2,1)}), bf16[128,2048]{1,0:T(8,128)(2,1)}) %all-reduce.11.cloned.1.call-update) | async-done | bytes 524304 | tf_op jit(solution)/shard_map/psum | solution.py:242
  557.5 38.9 %while.47 = (s32[]{:T(128)}, f32[128,4,2,128]{3,0,2,1:T(8,128)S(1)}, f32[2,1024,4,128]{3,2,1,0:T(4,128)}, f32[2,1024,4,128]{3,2,1,0:T(4,128)}, s32[2]{0:T(128)S(...) while((s32[]{:T(128)}, ...), condition=%wide.region_26.27_spmd.clone, body=%wide.region_23.26_spmd.clone.sunk | while | flops 1355940992 | bytes 54943664 | solution.py:300
  559.5 10.3 conditional.11
  569.8 7.7 copy_dynamic-update-slice_fusion.3
  579.5 10.0 conditional.11
  589.5 6.9 copy_dynamic-update-slice_fusion.3
  607.7 120.0 %reduce-scatter.5.cloned.1.call-done = f32[128,2048]{1,0:T(8,128)} async-done(((f32[2048,2048]{1,0:T(8,128)}), f32[128,2048]{1,0:T(8,128)}) %reduce-scatter.5.cloned.1.call-update) | async-done | bytes 1048592 | tf_op jit(solution)/shard_map/reduce_scatter | solution.py:223
  743.7 58.3 %reduce-scatter.9.cloned.1.call-done = f32[128,512]{1,0:T(8,128)} async-done(((f32[2048,512]{1,0:T(8,128)}), f32[128,512]{1,0:T(8,128)}) %reduce-scatter.9.cloned.1.call-update) | async-done | bytes 262160 | tf_op jit(solution)/shard_map/reduce_scatter | solution.py:306
  810.4 67.8 %reduce-scatter.11.cloned.1.call-done = f32[128,512]{1,0:T(8,128)} async-done(((f32[2048,512]{1,0:T(8,128)}), f32[128,512]{1,0:T(8,128)}) %reduce-scatter.11.cloned.1.call-update) | async-done | bytes 262160 | tf_op jit(solution)/shard_map/reduce_scatter | solution.py:307
  913.9 10.1 all-reduce.15.cloned.1.call-done
  925.5 49.6 %all-reduce = (f32[2048]{0:T(1024)}, f32[128]{0:T(128)}, f32[128]{0:T(128)}, f32[2048]{0:T(1024)}) all-reduce(f32[2048]{0:T(1024)S(1)} %get-tuple-element.661, bf16[128]{0:T(256)(128)(2,1)S(1)} %get-tuple-element.744, bf16[128]{0:T(256)(128)(2,1)S(1)} %get-tuple-element.745, ...), channel_id=1, replica_groups=mesh['tp'=2,'sp'=16] {'sp'}, use_global_device_ids=true, to_apply=%region_35.36 | all-reduce | flops 4352 | bytes 34304 | tf_op jit(solution)/shard_map/psum | solution.py:345
  978.8 396.2 %all-reduce.13.cloned.1.call-done = (f32[1024,2048]{1,0:T(8,128)}, f32[512,2048]{1,0:T(8,128)}, f32[512,2048]{1,0:T(8,128)}, f32[8,2048]{1,0:T(8,128)}, f32[2048,1024]{1,0:T(8,128)}) async-done(((f32[1024,2048]{1,0:T(8,128)}, f32[512,2048]{1,0:T(8,128)}, f32[512,2048]{1,0:T(8,128)}, f32[8,2048]{1,0:T(8,128)}, f32[2048,1024]{1,0:T(8,128)}), (f32[1024,2048]{1,0:T(8,128)}, f32[512,2048]{1,0:T(8,128)}, ...) | async-done | bytes 25231376 | tf_op jit(solution)/shard_map/psum | solution.py:345
  1375.0 8.0 copy.216
  (350 shorter events, 214.0 us)
Async XLA Ops:
  7.2 46.7 %all-gather.7.cloned.1.call-start = ((), (), s32[]{:S(2)}) async-start(), calls=%async_computation.5 | async-start | bytes 2228224 | tf_op jit(solution)/shard_map/all_gather | solution.py:148
  12.7 84.2 %all-gather.5.cloned.1.call-start = ((), (), s32[]{:S(2)}) async-start(), calls=%async_computation.4 | async-start | bytes 2228224 | tf_op jit(solution)/shard_map/all_gather | solution.py:147
  18.3 146.6 %all-reduce.9.cloned.1.call-start = ((), (), s32[]{:S(2)}) async-start(), calls=%async_computation.6 | async-start | bytes 1048576 | tf_op jit(solution)/shard_map/psum | solution.py:214
  24.9 528.8 %copy-start.42 = (f32[128,8]{0,1:T(8,128)}, f32[128,8]{0,1:T(8,128)S(1)}, u32[]{:S(2)}) copy-start(f32[128,8]{0,1:T(8,128)S(1)} %fusion.76) | copy-start | bytes 12292
  130.7 37.6 %copy-start.10 = (f32[4,2,128,128]{2,3,1,0:T(8,128)}, f32[4,2,128,128]{2,3,1,0:T(8,128)S(1)}, u32[]{:S(2)}) copy-start(f32[4,2,128,128]{2,3,1,0:T(8,128)S(1)} %copy.82) | copy-start | bytes 1572868
  136.1 105.6 %all-gather.11.cloned.1.call-start = ((), (), s32[]{:S(2)}) async-start(), calls=%async_computation.9 | async-start | bytes 8912896 | tf_op jit(solution)/shard_map/all_gather | solution.py:231
  136.7 181.0 %all-gather.9.cloned.1.call-start = ((), (), s32[]{:S(2)}) async-start(), calls=%async_computation.7 | async-start | bytes 8912896 | tf_op jit(solution)/shard_map/all_gather | solution.py:220
  166.2 381.9 %copy-start.53 = (f32[128]{0:T(128)}, f32[128]{0:T(128)S(1)}, u32[]{:S(2)}) copy-start(f32[128]{0:T(128)S(1)} %add_rsqrt_fusion.2) | copy-start | bytes 1540
  168.3 346.1 %reduce-scatter.7.cloned.1.call-start = ((), (), s32[]{:S(2)}) async-start(), calls=%async_computation.10 | async-start | bytes 17825792 | tf_op jit(solution)/shard_map/reduce_scatter | solution.py:239
  338.0 208.0 %all-reduce.11.cloned.1.call-start = ((), (), s32[]{:S(2)}) async-start(), calls=%async_computation.11 | async-start | bytes 1048576 | tf_op jit(solution)/shard_map/psum | solution.py:242
  516.5 211.2 %reduce-scatter.5.cloned.1.call-start = ((), (), s32[]{:S(2)}) async-start(), calls=%async_computation.8 | async-start | bytes 17825792 | tf_op jit(solution)/shard_map/reduce_scatter | solution.py:223
  526.1 19.9 %copy-start.4 = (bf16[128,2048]{1,0:T(8,128)(2,1)S(1)}, bf16[128,2048]{1,0:T(8,128)(2,1)}, u32[]{:S(2)}) copy-start(bf16[128,2048]{1,0:T(8,128)(2,1)} %all-reduce.9.cloned.1.call-done) | copy-start | bytes 1572868
  526.1 275.8 %reduce-scatter.9.cloned.1.call-start = ((), (), s32[]{:S(2)}) async-start(), calls=%async_computation.12 | async-start | bytes 4456448 | tf_op jit(solution)/shard_map/reduce_scatter | solution.py:306
  601.1 277.1 %reduce-scatter.11.cloned.1.call-start = ((), (), s32[]{:S(2)}) async-start(), calls=%async_computation.13 | async-start | bytes 4456448 | tf_op jit(solution)/shard_map/reduce_scatter | solution.py:307
  605.8 126.6 %copy-start.43 = (f32[128,8]{0,1:T(8,128)S(1)}, f32[128,8]{0,1:T(8,128)}, u32[]{:S(2)}) copy-start(f32[128,8]{0,1:T(8,128)} %copy-done.42) | copy-start | bytes 12292
  605.8 126.8 %copy-start.26 = (f32[128,64]{1,0:T(8,128)S(1)}, f32[128,64]{1,0:T(8,128)}, u32[]{:S(2)}) copy-start(f32[128,64]{1,0:T(8,128)} %copy-done.25) | copy-start | bytes 98308
  605.8 126.8 %copy-start.34 = (f32[128,64]{1,0:T(8,128)S(1)}, f32[128,64]{1,0:T(8,128)}, u32[]{:S(2)}) copy-start(f32[128,64]{1,0:T(8,128)} %get-tuple-element.777) | copy-start | bytes 98308
  605.9 318.1 %all-reduce.15.cloned.1.call-start = ((), (), s32[]{:S(2)}) async-start(), calls=%async_computation.15 | async-start | bytes 2097152 | tf_op jit(solution)/shard_map/psum | solution.py:226
  738.8 66.2 %copy-start.17 = (f32[128,4,128]{2,1,0:T(4,128)S(1)}, f32[128,4,128]{2,1,0:T(4,128)}, u32[]{:S(2)}) copy-start(f32[128,4,128]{2,1,0:T(4,128)} %copy-done.16) | copy-start | bytes 786436
  810.4 71.7 %copy-start.20 = (bf16[128,1024]{1,0:T(8,128)(2,1)S(1)}, bf16[128,1024]{1,0:T(8,128)(2,1)}, u32[]{:S(2)}) copy-start(bf16[128,1024]{1,0:T(8,128)(2,1)} %copy-done.19) | copy-start | bytes 786436
  881.8 493.2 %all-reduce.13.cloned.1.call-start = ((), (), s32[]{:S(2)}) async-start(), calls=%async_computation.14 | async-start | bytes 50462720 | tf_op jit(solution)/shard_map/psum | solution.py:345
  906.6 19.0 %copy-start.44 = (f32[2048]{0:T(1024)S(1)}, f32[2048]{0:T(1024)}, u32[]{:S(2)}) copy-start(f32[2048]{0:T(1024)} %get-tuple-element.659) | copy-start | bytes 24580
  906.6 68.6 %copy-start.55 = (f32[128]{0:T(128)S(1)}, f32[128]{0:T(128)}, u32[]{:S(2)}) copy-start(f32[128]{0:T(128)} %copy-done.53) | copy-start | bytes 1540
  906.6 68.6 %copy-start.61 = (f32[128]{0:T(128)S(1)}, f32[128]{0:T(128)}, u32[]{:S(2)}) copy-start(f32[128]{0:T(128)} %copy-done.59) | copy-start | bytes 1540
  (70 other events, 348.0 us)
Sparse Core Ops, SparseCore 0:
  12.8 41.0 all-gather.6
  56.6 40.1 all-gather.4
  136.2 28.6 all-reduce.8
  167.2 74.4 all-gather.10
  244.5 73.1 all-gather.8
  338.2 176.1 reduce-scatter.6
  517.3 28.6 all-reduce.10
  550.1 177.4 reduce-scatter.4
  732.1 69.8 reduce-scatter.8
  806.7 71.4 reduce-scatter.10
  881.9 41.9 all-reduce.14
  930.6 444.3 all-reduce.12
where the time goes:
time: 1410 us; the launch traced here: 1400 us
  waiting for transfers between devices  1080 us (77%)
  matrix products  123 us (9%)
  local copies, waits for them, and re-layouts  78 us (6%)
  blocking collectives  53.8 us (4%)
  other arithmetic  37.5 us (3%)
  between operations  15.6 us (1%)
    psum x1, waiting for transfers between devices, shards(): lax.psum((query_grad, key_grad, value_grad, headgate_grad, merge_grad, qu...  396 us
    reduce_scatter x1, waiting for transfers between devices, shards(): lax.psum_scatter(plain_dot(fold_stacked_grads, stacked_weights), 'sp', sc...  176 us
    reduce_scatter x1, waiting for transfers between devices, shards(): lax.psum_scatter(plain_dot(acts_all, down_weight), 'sp', scatter_dimensio...  120 us
    all_gather x1, waiting for transfers between devices, shards(): grads_low = lax.all_gather(out_cotangent, 'sp', axis=0, tiled=True)  73.3 us
    all_gather x1, waiting for transfers between devices, shards(): lax.all_gather(second_low, 'sp', axis=0, tiled=True)  68.4 us
    reduce_scatter x1, waiting for transfers between devices, shards(): lax.psum_scatter(value_terms, 'sp', scatter_dimension=0, tiled=True)  67.8 us
    reduce_scatter x1, waiting for transfers between devices, shards(): lax.psum_scatter(key_terms, 'sp', scatter_dimension=0, tiled=True)  58.3 us
    psum x1, blocking collectives, shards(): lax.psum((query_grad, key_grad, value_grad, headgate_grad, merge_grad, qu...  49.6 us
  transfers between devices with their start and end apart: 12, of which 12 were waited for; matrix products, arithmetic and copies ran while one was open for 11% of the time, Pallas kernels for 0%

commit v1 on v0

v1 whole, which is shorter than its diff:
```python
import math

import jax
import jax.numpy as jnp
from jax import lax
from jax.sharding import PartitionSpec as P

EPS = 1e-06
THETA = 1000000.0
NEG = -1e30
F32 = jnp.float32
BF16 = jnp.bfloat16


def right_dot(first_matrix, second_matrix, kind=F32):
    return lax.dot_general(
        first_matrix, second_matrix, (((1,), (1,)), ((), ())), preferred_element_type=F32
    ).astype(kind)


def plain_dot(first_matrix, second_matrix, kind=F32):
    return jnp.dot(first_matrix, second_matrix, preferred_element_type=F32).astype(kind)


def outer_dot(first_matrix, second_matrix, kind=F32):
    return lax.dot_general(
        first_matrix, second_matrix, (((0,), (0,)), ((), ())), preferred_element_type=F32
    ).astype(kind)


def normalize(values, gain_vector):
    inverse = lax.rsqrt(jnp.mean(values * values, axis=-1, keepdims=True) + EPS)
    return (values * inverse * gain_vector, inverse)


def normalize_back(values, inverse, gain_vector, upstream):
    weighted = upstream * gain_vector
    inner_mean = jnp.mean(weighted * values, axis=-1, keepdims=True)
    return (
        inverse * weighted - values * inverse * inverse * inverse * inner_mean,
        values * inverse * upstream,
    )


def rotary_tables(positions, head_width):
    half_width = head_width // 2
    frequency = THETA ** (-2.0 * jnp.arange(half_width, dtype=F32) / head_width)
    angles = positions.astype(F32)[:, None] * frequency[None, :]
    return (jnp.cos(angles)[:, None, :], jnp.sin(angles)[:, None, :])


def rotate(values, cosine_table, sine_table):
    half_width = values.shape[-1] // 2
    former = values[..., :half_width]
    latter = values[..., half_width:]
    return jnp.concatenate(
        [former * cosine_table - latter * sine_table, latter * cosine_table + former * sine_table],
        axis=-1,
    )


def swiglu_back(gate_pre, up_pre, grad_act):
    sigma = jax.nn.sigmoid(gate_pre)
    grad_gate = grad_act * up_pre * sigma * (1.0 + gate_pre * (1.0 - sigma))
    grad_up = grad_act * gate_pre * sigma
    return (grad_gate.astype(BF16), grad_up.astype(BF16))


def exchange(values, mask):
    size = lax.axis_size("sp")
    return lax.ppermute(values, "sp", [(i, i ^ mask) for i in range(size)])


def swap(values):
    return lax.ppermute(values, "tp", [(0, 1), (1, 0)])


def stack_rows(*pieces):
    return jnp.concatenate(pieces, axis=0)


def stack_columns(*pieces):
    return jnp.concatenate(pieces, axis=1)


def gather_over(values, masks):
    for mask in masks:
        values = stack_rows(values, exchange(values, mask))
    return values


def gather_direct(values, masks):
    return stack_rows(values, *[exchange(values, mask) for mask in masks])


def scatter_over(values, masks):
    for mask in reversed(masks):
        kept = values.shape[0] // 2
        arrived = exchange(values[kept:].astype(BF16), mask)
        values = values[:kept].astype(F32) + arrived.astype(F32)
    return values


def scatter_direct(values, masks):
    rows = values.shape[0] // (len(masks) + 1)
    total = values[:rows].astype(F32)
    for place, mask in enumerate(masks, start=1):
        piece = values[place * rows : (place + 1) * rows].astype(BF16)
        total = total + exchange(piece, mask).astype(F32)
    return total


def rows_at(values, start, count):
    return lax.dynamic_slice_in_dim(values, start, count, axis=0)


def columns_at(values, start, count):
    return lax.dynamic_slice_in_dim(values, start, count, axis=1)


def shards(
    tokens,
    item_lengths,
    first_gain,
    query_weight,
    key_weight,
    value_weight,
    headgate_weight,
    merge_weight,
    query_norm,
    key_norm,
    second_gain,
    gate_weight,
    up_weight,
    down_weight,
    out_cotangent,
):
    sp_size = lax.axis_size("sp")
    device = lax.axis_index("sp")
    side = lax.axis_index("tp")
    local_rows, width = tokens.shape
    half_rows = local_rows // 2
    head_width = query_norm.shape[0]
    local_heads = query_weight.shape[0] // head_width
    groups = key_weight.shape[0] // head_width
    group_size = local_heads // groups
    query_width = group_size * head_width
    score_scale = 1.0 / math.sqrt(head_width)

    bits = sp_size.bit_length() - 1
    group_step = 1 << (bits // 2)
    group_masks = [group_step * k for k in range(1, groups)]
    all_group_masks = [0] + group_masks
    group_bits = group_step * (groups - 1)
    rest = [1 << b for b in range(1, bits) if not (1 << b) & group_bits] + [1]
    rest_count = 1 << len(rest)
    rest_masks = [
        sum(mask for b, mask in enumerate(rest) if r >> b & 1) for r in range(rest_count)
    ]
    own_group = (device // group_step) % groups
    own_rest = sum(((device // mask) % 2) * (1 << b) for b, mask in enumerate(rest))

    residual = tokens.astype(F32)
    first_gain_f = first_gain.astype(F32)
    second_gain_f = second_gain.astype(F32)
    query_gain = query_norm.astype(F32)
    key_gain = key_norm.astype(F32)

    normed, first_inverse = normalize(residual, first_gain_f)
    normed_low = normed.astype(BF16)
    query_own = right_dot(normed_low, query_weight, BF16)
    key_own = right_dot(normed_low, key_weight, BF16)
    value_own = right_dot(normed_low, value_weight, BF16)
    gate_value = jax.nn.sigmoid(right_dot(normed_low, headgate_weight))

    def group_columns(values, group, count):
        return columns_at(values, group * count, count)

    arrived = []
    for mask_place, mask in enumerate(all_group_masks):
        group = own_group ^ mask_place
        piece = stack_columns(
            group_columns(query_own, group, query_width),
            group_columns(key_own, group, head_width),
            group_columns(value_own, group, head_width),
        )
        arrived.append(exchange(piece, mask) if mask else piece)
    head_rows = stack_rows(*arrived)
    owned = head_rows.shape[0]

    item_ends = jnp.cumsum(item_lengths)
    item_starts = item_ends - item_lengths

    def begins_of(row_index):
        return jnp.max(
            jnp.where(item_starts[None, :] <= row_index[:, None], item_starts[None, :], 0), axis=1
        )

    within = jnp.arange(local_rows, dtype=jnp.int32)

    def rows_from(mask):
        return (device ^ mask) * local_rows + within

    row_index = jnp.concatenate([rows_from(mask) for mask in all_group_masks])
    key_index = jnp.concatenate(
        [rows_from(outer ^ mask) for outer in rest_masks for mask in all_group_masks]
    )
    begins = begins_of(row_index)
    cosine_table, sine_table = rotary_tables(row_index - begins, head_width)

    query_raw = head_rows[:, :query_width].astype(F32).reshape(owned, group_size, head_width)
    key_raw = head_rows[:, query_width : query_width + head_width].astype(F32)
    key_raw = key_raw.reshape(owned, 1, head_width)
    query_unit, query_inverse = normalize(query_raw, query_gain)
    key_unit, key_inverse = normalize(key_raw, key_gain)
    queries = rotate(query_unit, cosine_table, sine_table).astype(BF16)
    keys_low = rotate(key_unit, cosine_table, sine_table).astype(BF16)[:, 0]
    pair_all = gather_over(stack_columns(keys_low, head_rows[:, query_width + head_width :]), rest)
    keys_all, values_all = pair_all[:, :head_width], pair_all[:, head_width:]

    valid = (key_index[None, :] >= begins[:, None]) & (key_index[None, :] <= row_index[:, None])
    scores = jnp.einsum("rgd,sd->grs", queries, keys_all, preferred_element_type=F32) * score_scale
    scores = jnp.where(valid, scores, NEG)
    highest = jnp.max(scores, axis=-1, keepdims=True)
    expo = jnp.where(valid, jnp.exp(scores - highest), 0.0)
    probs = expo / jnp.sum(expo, axis=-1, keepdims=True)
    probs_low = probs.astype(BF16)
    attended = jnp.einsum("grs,sd->rgd", probs_low, values_all, preferred_element_type=F32)

    def to_row_owner(values):
        pieces = [
            exchange(values[k * local_rows : (k + 1) * local_rows], mask)
            if mask
            else values[:local_rows]
            for k, mask in enumerate(all_group_masks)
        ]
        stacked = jnp.stack(pieces)
        return [
            lax.dynamic_index_in_dim(stacked, own_group ^ g, axis=0, keepdims=False)
            for g in range(groups)
        ]

    attended_low = attended.reshape(owned, query_width).astype(BF16)
    attended_rows = stack_columns(*to_row_owner(attended_low)).astype(F32)
    attended_rows = attended_rows.reshape(local_rows, local_heads, head_width)
    gated_low = (attended_rows * gate_value[..., None]).astype(BF16).reshape(local_rows, -1)
    attention_part = right_dot(gated_low, merge_weight)
    arrived_part = swap(rows_at(attention_part, (1 - side) * half_rows, half_rows).astype(BF16))
    attention_out = rows_at(attention_part, side * half_rows, half_rows) + arrived_part.astype(F32)
    hidden = rows_at(residual, side * half_rows, half_rows) + attention_out
    normed_second, second_inverse = normalize(hidden, second_gain_f)
    second_low = normed_second.astype(BF16)

    def units(weight):
        both = stack_rows(weight, swap(weight))
        return stack_rows(both, exchange(both, 1))

    gate_units, up_units, down_units = units(gate_weight), units(up_weight), units(down_weight)
    row_masks = rest[:-1]
    grad_half = rows_at(out_cotangent, side * half_rows, half_rows)
    grads_low = gather_over(gather_direct(grad_half, group_masks), row_masks)
    inputs_low = gather_over(gather_direct(second_low, group_masks), row_masks)
    gate_pre = right_dot(inputs_low, gate_units)
    up_pre = right_dot(inputs_low, up_units)
    act_low = (jax.nn.silu(gate_pre) * up_pre).astype(BF16)
    grad_act = right_dot(grads_low, down_units)
    grad_gate, grad_up = swiglu_back(gate_pre, up_pre, grad_act)

    def to_rows(values):
        return scatter_direct(scatter_over(values, row_masks), group_masks)

    grad_second = to_rows(plain_dot(grad_gate, gate_units) + plain_dot(grad_up, up_units))
    branch_out = to_rows(plain_dot(act_low, down_units))

    def own_units(first_matrix, second_matrix):
        values = outer_dot(first_matrix, second_matrix)
        kept = values.shape[0] // 2
        values = values[:kept] + exchange(values[kept:].astype(BF16), 1).astype(F32)
        kept = kept // 2
        return values[:kept] + swap(values[kept:].astype(BF16)).astype(F32)

    gate_acc = own_units(grad_gate, inputs_low)
    up_acc = own_units(grad_up, inputs_low)
    down_acc = own_units(act_low, grads_low)

    def both_sides(values):
        other = swap(values)
        return jnp.where(side == 0, stack_rows(values, other), stack_rows(other, values))

    layer_output = both_sides((hidden + branch_out).astype(BF16))
    grad_hidden_norm, second_terms = normalize_back(
        hidden, second_inverse, second_gain_f, grad_second
    )
    hidden_low = both_sides((grad_half.astype(F32) + grad_hidden_norm).astype(BF16))

    grad_gated = plain_dot(hidden_low, merge_weight).reshape(local_rows, local_heads, head_width)
    grad_attended_low = (grad_gated * gate_value[..., None]).astype(BF16).reshape(local_rows, -1)
    grad_logit_low = (
        jnp.sum(grad_gated * attended_rows, axis=-1) * gate_value * (1.0 - gate_value)
    ).astype(BF16)
    arrived = []
    for mask_place, mask in enumerate(all_group_masks):
        piece = group_columns(grad_attended_low, own_group ^ mask_place, query_width)
        arrived.append(exchange(piece, mask) if mask else piece)
    grad_grouped = stack_rows(*arrived).reshape(owned, group_size, head_width)
    row_delta = jnp.sum(grad_grouped.astype(F32) * attended, axis=-1).T
    grad_probs = jnp.einsum("rgd,sd->grs", grad_grouped, values_all, preferred_element_type=F32)
    grad_scores = (probs * (grad_probs - row_delta[..., None])).astype(BF16)
    grad_queries = (
        jnp.einsum("grs,sd->rgd", grad_scores, keys_all, preferred_element_type=F32) * score_scale
    )
    grad_keys = (
        jnp.einsum("grs,rgd->sd", grad_scores, queries, preferred_element_type=F32) * score_scale
    )
    grad_values = jnp.einsum("grs,rgd->sd", probs_low, grad_grouped, preferred_element_type=F32)
    pair_sum = scatter_over(stack_columns(grad_keys, grad_values), rest)

    grad_query_raw, query_gain_terms = normalize_back(
        query_raw, query_inverse, query_gain, rotate(grad_queries, cosine_table, -sine_table)
    )
    grad_key_unit = pair_sum[:, :head_width].reshape(owned, 1, head_width)
    grad_key_raw, key_gain_terms = normalize_back(
        key_raw, key_inverse, key_gain, rotate(grad_key_unit, cosine_table, -sine_table)
    )
    grad_head_rows = stack_columns(
        grad_query_raw.reshape(owned, query_width).astype(BF16),
        grad_key_raw.reshape(owned, head_width).astype(BF16),
        pair_sum[:, head_width:].astype(BF16),
    )

    back = to_row_owner(grad_head_rows)
    query_low = stack_columns(*[b[:, :query_width] for b in back])
    key_low = stack_columns(*[b[:, query_width : query_width + head_width] for b in back])
    value_low = stack_columns(*[b[:, query_width + head_width :] for b in back])
    input_part = (
        plain_dot(query_low, query_weight)
        + plain_dot(key_low, key_weight)
        + plain_dot(value_low, value_weight)
        + plain_dot(grad_logit_low, headgate_weight)
    ).astype(BF16)
    input_sum = input_part.astype(F32) + swap(input_part).astype(F32)
    grad_residual_norm, first_terms = normalize_back(
        residual, first_inverse, first_gain_f, input_sum
    )
    input_grad = hidden_low.astype(F32) + grad_residual_norm

    block = width // rest_count
    normed_half = rows_at(normed_low, side * half_rows, half_rows)
    normed_half = stack_columns(
        *[columns_at(normed_half, (own_rest ^ r) * block, block) for r in range(rest_count)]
    )
    normed_side = gather_direct(normed_half, group_masks)
    normed_owned = stack_rows(normed_side, swap(normed_side))
    halves = grad_head_rows.reshape(groups, 2, half_rows, -1)
    halves = jnp.where(side == 0, halves, halves[:, ::-1])
    halves = jnp.transpose(halves, (1, 0, 2, 3)).reshape(owned, -1)
    head_grads = outer_dot(halves, normed_owned)
    for mask in reversed(rest):
        kept = head_grads.shape[1] // 2
        head_grads = head_grads[:, :kept] + exchange(
            head_grads[:, kept:].astype(BF16), mask
        ).astype(F32)
    head_blocks = gather_over(gather_direct(head_grads.astype(BF16), group_masks), rest)
    head_blocks = head_blocks.reshape(sp_size, -1, block)
    query_grad = jnp.zeros(query_weight.shape, F32)
    key_grad = jnp.zeros(key_weight.shape, F32)
    value_grad = jnp.zeros(value_weight.shape, F32)
    for r in range(rest_count):
        for k in range(groups):
            piece = head_blocks[r * groups + k].astype(F32)
            group, column = own_group ^ k, (own_rest ^ r) * block
            query_grad = lax.dynamic_update_slice(
                query_grad, piece[:query_width], (group * query_width, column)
            )
            key_grad = lax.dynamic_update_slice(
                key_grad, piece[query_width : query_width + head_width], (group * head_width, column)
            )
            value_grad = lax.dynamic_update_slice(
                value_grad, piece[query_width + head_width :], (group * head_width, column)
            )

    strip = width // sp_size
    order = [outer ^ mask for outer in rest_masks for mask in all_group_masks]
    hidden_relative = stack_columns(
        *[columns_at(hidden_low, (device ^ mask) * strip, strip) for mask in order]
    )
    merge_part = outer_dot(hidden_relative, gated_low)
    merge_part = scatter_direct(scatter_over(merge_part, rest), group_masks)
    merge_blocks = gather_over(gather_direct(merge_part.astype(BF16), group_masks), rest)
    merge_grad = jnp.zeros(merge_weight.shape, F32)
    for place, mask in enumerate(order):
        merge_grad = lax.dynamic_update_slice(
            merge_grad,
            merge_blocks[place * strip : (place + 1) * strip].astype(F32),
            ((device ^ mask) * strip, 0),
        )

    headgate_part = outer_dot(grad_logit_low, normed_low)
    gains = jnp.concatenate(
        [
            jnp.sum(query_gain_terms, axis=(0, 1)),
            jnp.sum(key_gain_terms, axis=(0, 1)),
            jnp.zeros((width - 2 * head_width,), F32),
        ]
    )
    sides = jnp.stack([jnp.sum(second_terms, axis=0), gains])
    sides = sides + swap(sides)
    small = stack_rows(headgate_part, jnp.sum(first_terms, axis=0)[None], sides)
    for b in range(bits):
        small = small + exchange(small, 1 << b)

    return (
        layer_output,
        input_grad,
        small[local_heads],
        query_grad,
        key_grad,
        value_grad,
        small[:local_heads],
        merge_grad,
        small[local_heads + 2, :head_width],
        small[local_heads + 2, head_width : 2 * head_width],
        small[local_heads + 1],
        gate_acc,
        up_acc,
        down_acc,
    )


def solution(mesh):
    return jax.shard_map(
        shards,
        mesh=mesh,
        in_specs=(
            P("sp", None),
            P(),
            P(),
            P("tp", None),
            P("tp", None),
            P("tp", None),
            P("tp", None),
            P(None, "tp"),
            P(),
            P(),
            P(),
            P(("tp", "sp"), None),
            P(("tp", "sp"), None),
            P(("tp", "sp"), None),
            P("sp", None),
        ),
        out_specs=(
            P("sp", None),
            P("sp", None),
            P(),
            P("tp", None),
            P("tp", None),
            P("tp", None),
            P("tp", None),
            P(None, "tp"),
            P(),
            P(),
            P(),
            P(("tp", "sp"), None),
            P(("tp", "sp"), None),
            P(("tp", "sp"), None),
        ),
        check_vma=False,
    )
```

time: 1410 us -> 587 us (0.42)
  waiting for transfers between devices: 1080 us -> 226 us
  starting transfers between devices: 1.6 us -> 108 us
  matrix products: 123 us -> 58.5 us
  other arithmetic: 37.5 us -> 91.3 us
  blocking collectives: 53.8 us -> 0 us
    psum x4 -> x0, waiting for transfers between devices: 454 us -> none  [the longest x1 396 us: shards(): lax.psum((query_grad, key_grad, value_grad, headgate_grad, merge_grad, qu...]
    reduce_scatter x4 -> x0, waiting for transfers between devices: 422 us -> none  [the longest x1 176 us: shards(): lax.psum_scatter(plain_dot(fold_stacked_grads, stacked_weights), 'sp', sc...]
    ppermute x0 -> x74, waiting for transfers between devices: none -> 226 us  [the longest x62 201 us: exchange(): return lax.ppermute(values, 'sp', [(i, i ^ mask) for i in range(size)])]
    all_gather x4 -> x0, waiting for transfers between devices: 207 us -> none  [the longest x1 73.3 us: shards(): grads_low = lax.all_gather(out_cotangent, 'sp', axis=0, tiled=True)]
    ppermute x0 -> x74, starting transfers between devices: none -> 108 us  [the longest x62 99.1 us: exchange(): return lax.ppermute(values, 'sp', [(i, i ^ mask) for i in range(size)])]
    psum x2 -> x0, blocking collectives: 53.8 us -> none  [the longest x1 49.6 us: shards(): lax.psum((query_grad, key_grad, value_grad, headgate_grad, merge_grad, qu...]
    dot_general x21 -> x13, matrix products: 57.9 us -> 23.1 us  [the longest x8 9.06 us: plain_dot(): jnp.dot(first_matrix, second_matrix, preferred_element_type=F32)]
    dot_general x8 -> x6, matrix products: 33.2 us -> 9.41 us  [outer_dot(): lax.dot_general(first_matrix, second_matrix, (((0,), (0,)), ((), ())), pr...]
  transfers between devices with their start and end apart: 12 -> 74, of which waited for: 12 -> 30; matrix products, arithmetic and copies ran while one was open for 11% -> 37% of each run, Pallas kernels for 0% -> 0%
where the time goes in v1:
time: 587 us; the launch traced here: 578 us
  waiting for transfers between devices  226 us (39%)
  starting transfers between devices  108 us (18%)
  other arithmetic  91.3 us (16%)
  local copies, waits for them, and re-layouts  90 us (15%)
  matrix products  58.5 us (10%)
    ppermute x62, waiting for transfers between devices, exchange(): return lax.ppermute(values, 'sp', [(i, i ^ mask) for i in range(size)])  201 us
    ppermute x62, starting transfers between devices, exchange(): return lax.ppermute(values, 'sp', [(i, i ^ mask) for i in range(size)])  99.1 us
    unnamed x221, local copies, waits for them, and re-layouts  42.3 us
    ppermute x12, waiting for transfers between devices, swap(): return lax.ppermute(values, 'tp', [(0, 1), (1, 0)])  24.7 us
    dot_general x8, matrix products, right_dot(): lax.dot_general(first_matrix, second_matrix, (((1,), (1,)), ((), ())), pr...  16.5 us
    concatenate x12, other arithmetic, stack_rows(): return jnp.concatenate(pieces, axis=0)  13.4 us
  transfers between devices with their start and end apart: 74, of which 30 were waited for; matrix products, arithmetic and copies ran while one was open for 37% of the time, Pallas kernels for 0%

profile of v1, /device:TPU:17, one launch (start us, length us, event | category | flops | bytes accessed | tf_op | source)
XLA Modules:
  0.0 578.3 jit_solution(16601908554999676696)
XLA Ops:
  80.0 14.4 %collective-permute-done.49 = bf16[64,2048]{1,0:T(8,128)(2,1)S(1)} collective-permute-done((bf16[64,2048]{1,0:T(8,128)(2,1)}, bf16[64,2048]{1,0:T(8,128)(2,1)S(1)}, u32[]{:S(2)}, u32[]{:S(2)}) %collective-permute-start.49) | collective-permute-done | bytes 262176 | tf_op jit(solution)/shard_map/ppermute | solution.py:71
  109.7 9.5 %fusion.116 = (f32[2,512]{1,0:T(2,128)S(1)}, f32[2,512,2048]{1,2,0:T(8,128)}) fusion(pred[512,2048]{0,1:T(8,128)(4,1)} %compare_and_fusion, bf16[2048,256]{1,0:T(8,128)(2,1)} %pad_maximum_fusion.5, bf16[512,2,64]{2,0,1:T(8,128)(2,1)} %get-tuple-element.102, bf16[512,2,64]{2,0,1:T(8,128)(2,1)} %get-tuple-element.101), kind=kOutput, calls=%fused_computation.432 | convolution fusion | flops 547883008 | bytes 11538432 | tf_op jit(solution)/shard_map/sub | solution.py:225
  119.2 4.7 fusion.7
  147.9 14.2 %collective-permute-done.8 = bf16[64,2048]{1,0:T(8,128)(2,1)S(1)} collective-permute-done((bf16[64,2048]{1,0:T(8,128)(2,1)S(1)}, bf16[64,2048]{1,0:T(8,128)(2,1)S(1)}, u32[]{:S(2)}, u32[]{:S(2)}) %collective-permute-start.8) | collective-permute-done | bytes 262176 | tf_op jit(solution)/shard_map/ppermute | solution.py:75
  168.9 4.3 collective-permute-start.14
  174.6 13.9 %collective-permute-done.11 = bf16[64,2048]{1,0:T(8,128)(2,1)S(1)} collective-permute-done((bf16[64,2048]{1,0:T(8,128)(2,1)S(1)}, bf16[64,2048]{1,0:T(8,128)(2,1)S(1)}, u32[]{:S(2)}, u32[]{:S(2)}) %collective-permute-start.11) | collective-permute-done | bytes 262176 | tf_op jit(solution)/shard_map/ppermute | solution.py:71
  195.6 15.6 %collective-permute-done.12 = bf16[256,2048]{1,0:T(8,128)(2,1)S(1)} collective-permute-done((bf16[256,2048]{1,0:T(8,128)(2,1)S(1)}, bf16[256,2048]{1,0:T(8,128)(2,1)S(1)}, u32[]{:S(2)}, u32[]{:S(2)}) %collective-permute-start.12) | collective-permute-done | bytes 1048608 | tf_op jit(solution)/shard_map/ppermute | solution.py:71
  233.3 8.1 %collective-permute-done.28 = bf16[256,2048]{1,0:T(8,128)(2,1)} collective-permute-done((bf16[256,2048]{1,0:T(8,128)(2,1)S(1)}, bf16[256,2048]{1,0:T(8,128)(2,1)}, u32[]{:S(2)}, u32[]{:S(2)}) %collective-permute-start.28) | collective-permute-done | bytes 1048608 | tf_op jit(solution)/shard_map/ppermute | solution.py:71
  243.3 20.4 %collective-permute-done.19 = bf16[256,2048]{1,0:T(8,128)(2,1)S(1)} collective-permute-done((bf16[256,2048]{1,0:T(8,128)(2,1)S(1)}, bf16[256,2048]{1,0:T(8,128)(2,1)S(1)}, u32[]{:S(2)}, u32[]{:S(2)}) %collective-permute-start.19) | collective-permute-done | bytes 1048608 | tf_op jit(solution)/shard_map/ppermute | solution.py:71
  272.8 16.4 %collective-permute-start.72 = (bf16[384,2048]{1,0:T(8,128)(2,1)S(1)}, bf16[384,2048]{1,0:T(8,128)(2,1)S(1)}, u32[]{:S(2)}, u32[]{:S(2)}) collective-permute-start(bf16[384,2048]{1,0:T(8,128)(2,1)S(1)} %slice.996), channel_id=1, source_target_pairs={{0,1},{1,0},{2,3},{3,2},{4,5},{5,4},{6,7},{7,6},{8,9},{9,8},{10,11... | collective-permute-start | bytes 4718600 | tf_op jit(solution)/shard_map/ppermute | solution.py:71
  332.7 7.1 %collective-permute-start.58 = (bf16[1024,1024]{1,0:T(8,128)(2,1)}, bf16[1024,1024]{1,0:T(8,128)(2,1)}, u32[]{:S(2)}, u32[]{:S(2)}) collective-permute-start(bf16[1024,1024]{1,0:T(8,128)(2,1)} %slice.995), channel_id=1, source_target_pairs={{0,1},{1,0},{2,3},{3,2},{4,5},{5,4},{6,7},{7,6},{8,9},{9,8},{10,11... | collective-permute-start | bytes 6291464 | tf_op jit(solution)/shard_map/ppermute | solution.py:71
  348.0 5.3 fusion.2
  378.1 5.3 collective-permute-done.40
  392.9 7.8 %collective-permute-done.41 = bf16[128,2048]{1,0:T(8,128)(2,1)S(1)} collective-permute-done((bf16[128,2048]{1,0:T(8,128)(2,1)S(1)}, bf16[128,2048]{1,0:T(8,128)(2,1)S(1)}, u32[]{:S(2)}, u32[]{:S(2)}) %collective-permute-start.41) | collective-permute-done | bytes 524320 | tf_op jit(solution)/shard_map/ppermute | solution.py:75
  427.2 5.0 collective-permute-done.52
  432.5 5.8 collective-permute-start.53
  441.7 15.5 %collective-permute-done.53 = bf16[512,512]{1,0:T(8,128)(2,1)S(1)} collective-permute-done((bf16[512,512]{1,0:T(8,128)(2,1)S(1)}, bf16[512,512]{1,0:T(8,128)(2,1)S(1)}, u32[]{:S(2)}, u32[]{:S(2)}) %collective-permute-start.53) | collective-permute-done | bytes 524320 | tf_op jit(solution)/shard_map/ppermute | solution.py:71
  457.3 26.0 %collective-permute-done.55 = bf16[512,512]{1,0:T(8,128)(2,1)S(1)} collective-permute-done((bf16[512,512]{1,0:T(8,128)(2,1)S(1)}, bf16[512,512]{1,0:T(8,128)(2,1)S(1)}, u32[]{:S(2)}, u32[]{:S(2)}) %collective-permute-start.55) | collective-permute-done | bytes 524320 | tf_op jit(solution)/shard_map/ppermute | solution.py:71
  490.2 10.7 %collective-permute-done.62 = bf16[128,1024]{1,0:T(8,128)(2,1)S(1)} collective-permute-done((bf16[128,1024]{1,0:T(8,128)(2,1)S(1)}, bf16[128,1024]{1,0:T(8,128)(2,1)S(1)}, u32[]{:S(2)}, u32[]{:S(2)}) %collective-permute-start.62) | collective-permute-done | bytes 262176 | tf_op jit(solution)/shard_map/ppermute | solution.py:71
  501.0 5.4 collective-permute-done.61
  512.0 6.3 %collective-permute-done.63 = bf16[128,1024]{1,0:T(8,128)(2,1)S(1)} collective-permute-done((bf16[128,1024]{1,0:T(8,128)(2,1)S(1)}, bf16[128,1024]{1,0:T(8,128)(2,1)S(1)}, u32[]{:S(2)}, u32[]{:S(2)}) %collective-permute-start.63) | collective-permute-done | bytes 262176 | tf_op jit(solution)/shard_map/ppermute | solution.py:71
  519.6 12.8 %collective-permute-done.65 = bf16[128,1024]{1,0:T(8,128)(2,1)S(1)} collective-permute-done((bf16[128,1024]{1,0:T(8,128)(2,1)S(1)}, bf16[128,1024]{1,0:T(8,128)(2,1)S(1)}, u32[]{:S(2)}, u32[]{:S(2)}) %collective-permute-start.65) | collective-permute-done | bytes 262176 | tf_op jit(solution)/shard_map/ppermute | solution.py:71
  533.3 21.3 %collective-permute-done.66 = bf16[512,1024]{1,0:T(8,128)(2,1)S(1)} collective-permute-done((bf16[512,1024]{1,0:T(8,128)(2,1)S(1)}, bf16[512,1024]{1,0:T(8,128)(2,1)S(1)}, u32[]{:S(2)}, u32[]{:S(2)}) %collective-permute-start.66) | collective-permute-done | bytes 1048608 | tf_op jit(solution)/shard_map/ppermute | solution.py:71
  563.9 4.3 collective-permute-done.57
  (608 shorter events, 313.8 us)
Async XLA Ops:
  2.6 64.1 %collective-permute-start.24 = (bf16[64,2048]{1,0:T(8,128)(2,1)}, bf16[64,2048]{1,0:T(8,128)(2,1)}, u32[]{:S(2)}, u32[]{:S(2)}) collective-permute-start(bf16[64,2048]{1,0:T(8,128)(2,1)} %get-tuple-element.30), channel_id=1, source_target_pairs={{0,4},{1,5},{2,6},{3,7},{4,0},{5,1},{6,2},{7,3},{8,12},{9,13},{10,... | collective-permute-start | bytes 786440 | tf_op jit(solution)/shard_map/ppermute | solution.py:71
  3.9 67.0 %collective-permute-start.25 = (bf16[64,2048]{1,0:T(8,128)(2,1)}, bf16[64,2048]{1,0:T(8,128)(2,1)}, u32[]{:S(2)}, u32[]{:S(2)}) collective-permute-start(bf16[64,2048]{1,0:T(8,128)(2,1)} %get-tuple-element.30), channel_id=1, source_target_pairs={{0,8},{1,9},{2,10},{3,11},{4,12},{5,13},{6,14},{7,15},{8,0},{9,1},... | collective-permute-start | bytes 786440 | tf_op jit(solution)/shard_map/ppermute | solution.py:71
  15.7 30.0 %collective-permute-start.2 = (bf16[128,512]{1,0:T(8,128)(2,1)}, bf16[128,512]{1,0:T(8,128)(2,1)S(1)}, u32[]{:S(2)}, u32[]{:S(2)}) collective-permute-start(bf16[128,512]{1,0:T(8,128)(2,1)} %pad_maximum_fusion.29), channel_id=1, source_target_pairs={{0,12},{1,13},{2,14},{3,15},{4,8},{5,9},{6,10},{7,11},{8,4},{9,5},... | collective-permute-start | bytes 393224 | tf_op jit(solution)/shard_map/ppermute | solution.py:71
  17.6 29.2 %collective-permute-start.1 = (bf16[128,512]{1,0:T(8,128)(2,1)}, bf16[128,512]{1,0:T(8,128)(2,1)S(1)}, u32[]{:S(2)}, u32[]{:S(2)}) collective-permute-start(bf16[128,512]{1,0:T(8,128)(2,1)} %pad_maximum_fusion.28), channel_id=1, source_target_pairs={{0,8},{1,9},{2,10},{3,11},{4,12},{5,13},{6,14},{7,15},{8,0},{9,1},... | collective-permute-start | bytes 393224 | tf_op jit(solution)/shard_map/ppermute | solution.py:71
  19.3 28.7 %collective-permute-start = (bf16[128,512]{1,0:T(8,128)(2,1)}, bf16[128,512]{1,0:T(8,128)(2,1)S(1)}, u32[]{:S(2)}, u32[]{:S(2)}) collective-permute-start(bf16[128,512]{1,0:T(8,128)(2,1)} %pad_maximum_fusion.27), channel_id=1, source_target_pairs={{0,4},{1,5},{2,6},{3,7},{4,0},{5,1},{6,2},{7,3},{8,12},{9,13},{10,... | collective-permute-start | bytes 393224 | tf_op jit(solution)/shard_map/ppermute | solution.py:71
  45.6 27.0 %collective-permute-start.26 = (bf16[64,2048]{1,0:T(8,128)(2,1)}, bf16[64,2048]{1,0:T(8,128)(2,1)}, u32[]{:S(2)}, u32[]{:S(2)}) collective-permute-start(bf16[64,2048]{1,0:T(8,128)(2,1)} %get-tuple-element.30), channel_id=1, source_target_pairs={{0,12},{1,13},{2,14},{3,15},{4,8},{5,9},{6,10},{7,11},{8,4},{9,5},... | collective-permute-start | bytes 786440 | tf_op jit(solution)/shard_map/ppermute | solution.py:71
  46.8 54.8 %collective-permute-start.17 = (bf16[192,2048]{1,0:T(8,128)(2,1)}, bf16[192,2048]{1,0:T(8,128)(2,1)}, u32[]{:S(2)}, u32[]{:S(2)}) collective-permute-start(bf16[192,2048]{1,0:T(8,128)(2,1)} %param.28), channel_id=1, source_target_pairs={{0,16},{16,0},{1,17},{17,1},{2,18},{18,2},{3,19},{19,3},{4,20},{20... | collective-permute-start | bytes 2359304 | tf_op jit(solution)/shard_map/ppermute | solution.py:75
  48.0 58.1 %collective-permute-start.15 = (bf16[192,2048]{1,0:T(8,128)(2,1)}, bf16[192,2048]{1,0:T(8,128)(2,1)}, u32[]{:S(2)}, u32[]{:S(2)}) collective-permute-start(bf16[192,2048]{1,0:T(8,128)(2,1)} %param.27), channel_id=1, source_target_pairs={{0,16},{16,0},{1,17},{17,1},{2,18},{18,2},{3,19},{19,3},{4,20},{20... | collective-permute-start | bytes 2359304 | tf_op jit(solution)/shard_map/ppermute | solution.py:75
  77.9 66.9 %collective-permute-start.13 = (bf16[192,2048]{1,0:T(8,128)(2,1)}, bf16[192,2048]{1,0:T(8,128)(2,1)}, u32[]{:S(2)}, u32[]{:S(2)}) collective-permute-start(bf16[192,2048]{1,0:T(8,128)(2,1)} %param.26), channel_id=1, source_target_pairs={{0,16},{16,0},{1,17},{17,1},{2,18},{18,2},{3,19},{19,3},{4,20},{20... | collective-permute-start | bytes 2359304 | tf_op jit(solution)/shard_map/ppermute | solution.py:75
  94.4 70.2 %collective-permute-start.27 = (bf16[256,2048]{1,0:T(8,128)(2,1)}, bf16[256,2048]{1,0:T(8,128)(2,1)}, u32[]{:S(2)}, u32[]{:S(2)}) collective-permute-start(bf16[256,2048]{1,0:T(8,128)(2,1)} %pad_maximum_fusion.7), channel_id=1, source_target_pairs={{0,2},{1,3},{2,0},{3,1},{4,6},{5,7},{6,4},{7,5},{8,10},{9,11},{10,... | collective-permute-start | bytes 3145736 | tf_op jit(solution)/shard_map/ppermute | solution.py:71
  132.2 33.1 %collective-permute-start.50 = (bf16[256,2048]{1,0:T(8,128)(2,1)}, bf16[256,2048]{1,0:T(8,128)(2,1)}, u32[]{:S(2)}, u32[]{:S(2)}) collective-permute-start(bf16[256,2048]{1,0:T(8,128)(2,1)} %pad_maximum_fusion.8), channel_id=1, source_target_pairs={{0,16},{16,0},{1,17},{17,1},{2,18},{18,2},{3,19},{19,3},{4,20},{20... | collective-permute-start | bytes 3145736 | tf_op jit(solution)/shard_map/ppermute | solution.py:75
  133.8 56.2 %collective-permute-start.18 = (bf16[384,2048]{1,0:T(8,128)(2,1)}, bf16[384,2048]{1,0:T(8,128)(2,1)}, u32[]{:S(2)}, u32[]{:S(2)}) collective-permute-start(bf16[384,2048]{1,0:T(8,128)(2,1)} %pad_maximum_fusion.3), channel_id=1, source_target_pairs={{0,1},{1,0},{2,3},{3,2},{4,5},{5,4},{6,7},{7,6},{8,9},{9,8},{10,11... | collective-permute-start | bytes 4718600 | tf_op jit(solution)/shard_map/ppermute | solution.py:71
  135.0 56.5 %collective-permute-start.16 = (bf16[384,2048]{1,0:T(8,128)(2,1)}, bf16[384,2048]{1,0:T(8,128)(2,1)}, u32[]{:S(2)}, u32[]{:S(2)}) collective-permute-start(bf16[384,2048]{1,0:T(8,128)(2,1)} %pad_maximum_fusion.2), channel_id=1, source_target_pairs={{0,1},{1,0},{2,3},{3,2},{4,5},{5,4},{6,7},{7,6},{8,9},{9,8},{10,11... | collective-permute-start | bytes 4718600 | tf_op jit(solution)/shard_map/ppermute | solution.py:71
  224.7 39.0 %collective-permute-start.19 = (bf16[256,2048]{1,0:T(8,128)(2,1)S(1)}, bf16[256,2048]{1,0:T(8,128)(2,1)S(1)}, u32[]{:S(2)}, u32[]{:S(2)}) collective-permute-start(bf16[256,2048]{1,0:T(8,128)(2,1)S(1)} %slice.1002), channel_id=1, source_target_pairs={{0,2},{1,3},{2,0},{3,1},{4,6},{5,7},{6,4},{7,5},{8,10},{9,11},{10,... | collective-permute-start | bytes 3145736 | tf_op jit(solution)/shard_map/ppermute | solution.py:71
  225.2 67.5 %collective-permute-start.68 = (bf16[384,2048]{1,0:T(8,128)(2,1)S(1)}, bf16[384,2048]{1,0:T(8,128)(2,1)}, u32[]{:S(2)}, u32[]{:S(2)}) collective-permute-start(bf16[384,2048]{1,0:T(8,128)(2,1)S(1)} %slice.998), channel_id=1, source_target_pairs={{0,1},{1,0},{2,3},{3,2},{4,5},{5,4},{6,7},{7,6},{8,9},{9,8},{10,11... | collective-permute-start | bytes 4718600 | tf_op jit(solution)/shard_map/ppermute | solution.py:71
  231.1 65.8 %collective-permute-start.70 = (bf16[384,2048]{1,0:T(8,128)(2,1)S(1)}, bf16[384,2048]{1,0:T(8,128)(2,1)S(1)}, u32[]{:S(2)}, u32[]{:S(2)}) collective-permute-start(bf16[384,2048]{1,0:T(8,128)(2,1)S(1)} %slice.997), channel_id=1, source_target_pairs={{0,1},{1,0},{2,3},{3,2},{4,5},{5,4},{6,7},{7,6},{8,9},{9,8},{10,11... | collective-permute-start | bytes 4718600 | tf_op jit(solution)/shard_map/ppermute | solution.py:71
  291.3 34.3 %collective-permute-start.23 = (bf16[64,2048]{1,0:T(8,128)(2,1)}, bf16[64,2048]{1,0:T(8,128)(2,1)}, u32[]{:S(2)}, u32[]{:S(2)}) collective-permute-start(bf16[64,2048]{1,0:T(8,128)(2,1)} %get-tuple-element.122), channel_id=1, source_target_pairs={{0,16},{16,0},{1,17},{17,1},{2,18},{18,2},{3,19},{19,3},{4,20},{20... | collective-permute-start | bytes 786440 | tf_op jit(solution)/shard_map/ppermute | solution.py:75
  295.9 71.2 %collective-permute-start.69 = (bf16[192,2048]{1,0:T(8,128)(2,1)}, bf16[192,2048]{1,0:T(8,128)(2,1)}, u32[]{:S(2)}, u32[]{:S(2)}) collective-permute-start(bf16[192,2048]{1,0:T(8,128)(2,1)} %slice.1005), channel_id=1, source_target_pairs={{0,16},{16,0},{1,17},{17,1},{2,18},{18,2},{3,19},{19,3},{4,20},{20... | collective-permute-start | bytes 2359304 | tf_op jit(solution)/shard_map/ppermute | solution.py:75
  298.7 70.8 %collective-permute-start.71 = (bf16[192,2048]{1,0:T(8,128)(2,1)}, bf16[192,2048]{1,0:T(8,128)(2,1)}, u32[]{:S(2)}, u32[]{:S(2)}) collective-permute-start(bf16[192,2048]{1,0:T(8,128)(2,1)} %slice.1004), channel_id=1, source_target_pairs={{0,16},{16,0},{1,17},{17,1},{2,18},{18,2},{3,19},{19,3},{4,20},{20... | collective-permute-start | bytes 2359304 | tf_op jit(solution)/shard_map/ppermute | solution.py:75
  331.6 58.5 %collective-permute-start.73 = (bf16[192,2048]{1,0:T(8,128)(2,1)}, bf16[192,2048]{1,0:T(8,128)(2,1)}, u32[]{:S(2)}, u32[]{:S(2)}) collective-permute-start(bf16[192,2048]{1,0:T(8,128)(2,1)} %slice.1003), channel_id=1, source_target_pairs={{0,16},{16,0},{1,17},{17,1},{2,18},{18,2},{3,19},{19,3},{4,20},{20... | collective-permute-start | bytes 2359304 | tf_op jit(solution)/shard_map/ppermute | solution.py:75
  332.7 91.5 %collective-permute-start.58 = (bf16[1024,1024]{1,0:T(8,128)(2,1)}, bf16[1024,1024]{1,0:T(8,128)(2,1)}, u32[]{:S(2)}, u32[]{:S(2)}) collective-permute-start(bf16[1024,1024]{1,0:T(8,128)(2,1)} %slice.995), channel_id=1, source_target_pairs={{0,1},{1,0},{2,3},{3,2},{4,5},{5,4},{6,7},{7,6},{8,9},{9,8},{10,11... | collective-permute-start | bytes 6291464 | tf_op jit(solution)/shard_map/ppermute | solution.py:71
  426.8 58.5 %collective-permute-start.59 = (bf16[512,1024]{1,0:T(8,128)(2,1)S(1)}, bf16[512,1024]{1,0:T(8,128)(2,1)S(1)}, u32[]{:S(2)}, u32[]{:S(2)}) collective-permute-start(bf16[512,1024]{1,0:T(8,128)(2,1)S(1)} %slice.999), channel_id=1, source_target_pairs={{0,2},{1,3},{2,0},{3,1},{4,6},{5,7},{6,4},{7,5},{8,10},{9,11},{10,... | collective-permute-start | bytes 3145736 | tf_op jit(solution)/shard_map/ppermute | solution.py:71
  438.7 44.5 %collective-permute-start.55 = (bf16[512,512]{1,0:T(8,128)(2,1)S(1)}, bf16[512,512]{1,0:T(8,128)(2,1)S(1)}, u32[]{:S(2)}, u32[]{:S(2)}) collective-permute-start(bf16[512,512]{1,0:T(8,128)(2,1)S(1)} %get-tuple-element.25), channel_id=1, source_target_pairs={{0,12},{1,13},{2,14},{3,15},{4,8},{5,9},{6,10},{7,11},{8,4},{9,5},... | collective-permute-start | bytes 1572872 | tf_op jit(solution)/shard_map/ppermute | solution.py:71
  483.4 75.1 %collective-permute-start.56 = (bf16[2048,512]{1,0:T(8,128)(2,1)S(1)}, bf16[2048,512]{1,0:T(8,128)(2,1)S(1)}, u32[]{:S(2)}, u32[]{:S(2)}) collective-permute-start(bf16[2048,512]{1,0:T(8,128)(2,1)S(1)} %pad_maximum_fusion), channel_id=1, source_target_pairs={{0,2},{1,3},{2,0},{3,1},{4,6},{5,7},{6,4},{7,5},{8,10},{9,11},{10,... | collective-permute-start | bytes 6291464 | tf_op jit(solution)/shard_map/ppermute | solution.py:71
  (143 other events, 1458.0 us)

commit v2 on v1

v2 whole, which is shorter than its diff:
```python
import math

import jax
import jax.numpy as jnp
from jax import lax
from jax.experimental import pallas as pl
from jax.experimental.pallas import tpu as pltpu
from jax.sharding import PartitionSpec as P

EPS = 1e-06
THETA = 1000000.0
NEG = -1e30
F32 = jnp.float32
BF16 = jnp.bfloat16


def right_dot(first_matrix, second_matrix, kind=F32):
    return lax.dot_general(
        first_matrix, second_matrix, (((1,), (1,)), ((), ())), preferred_element_type=F32
    ).astype(kind)


def plain_dot(first_matrix, second_matrix, kind=F32):
    return jnp.dot(first_matrix, second_matrix, preferred_element_type=F32).astype(kind)


def outer_dot(first_matrix, second_matrix, kind=F32):
    return lax.dot_general(
        first_matrix, second_matrix, (((0,), (0,)), ((), ())), preferred_element_type=F32
    ).astype(kind)


def normalize(values, gain_vector):
    inverse = lax.rsqrt(jnp.mean(values * values, axis=-1, keepdims=True) + EPS)
    return (values * inverse * gain_vector, inverse)


def normalize_back(values, inverse, gain_vector, upstream):
    weighted = upstream * gain_vector
    inner_mean = jnp.mean(weighted * values, axis=-1, keepdims=True)
    return (
        inverse * weighted - values * inverse * inverse * inverse * inner_mean,
        values * inverse * upstream,
    )


def rotary_tables(positions, head_width):
    half_width = head_width // 2
    frequency = THETA ** (-2.0 * jnp.arange(half_width, dtype=F32) / head_width)
    angles = positions.astype(F32)[:, None] * frequency[None, :]
    return (jnp.cos(angles)[:, None, :], jnp.sin(angles)[:, None, :])


def rotate(values, cosine_table, sine_table):
    half_width = values.shape[-1] // 2
    former = values[..., :half_width]
    latter = values[..., half_width:]
    return jnp.concatenate(
        [former * cosine_table - latter * sine_table, latter * cosine_table + former * sine_table],
        axis=-1,
    )


def swiglu_back(gate_pre, up_pre, grad_act):
    sigma = jax.nn.sigmoid(gate_pre)
    grad_gate = grad_act * up_pre * sigma * (1.0 + gate_pre * (1.0 - sigma))
    grad_up = grad_act * gate_pre * sigma
    return (grad_gate.astype(BF16), grad_up.astype(BF16))


def exchange(values, mask):
    size = lax.axis_size("sp")
    return lax.ppermute(values, "sp", [(i, i ^ mask) for i in range(size)])


def swap(values):
    return lax.ppermute(values, "tp", [(0, 1), (1, 0)])


def stack_rows(*pieces):
    return jnp.concatenate(pieces, axis=0)


def stack_columns(*pieces):
    return jnp.concatenate(pieces, axis=1)


def gather_over(values, masks):
    for mask in masks:
        values = stack_rows(values, exchange(values, mask))
    return values


def gather_direct(values, masks):
    return stack_rows(values, *[exchange(values, mask) for mask in masks])


def scatter_over(values, masks):
    for mask in reversed(masks):
        kept = values.shape[0] // 2
        arrived = exchange(values[kept:].astype(BF16), mask)
        values = values[:kept].astype(F32) + arrived.astype(F32)
    return values


def scatter_direct(values, masks):
    rows = values.shape[0] // (len(masks) + 1)
    total = values[:rows].astype(F32)
    for place, mask in enumerate(masks, start=1):
        piece = values[place * rows : (place + 1) * rows].astype(BF16)
        total = total + exchange(piece, mask).astype(F32)
    return total


def rows_at(values, start, count):
    return lax.dynamic_slice_in_dim(values, start, count, axis=0)


def columns_at(values, start, count):
    return lax.dynamic_slice_in_dim(values, start, count, axis=1)


def after_all(values, *others):
    return lax.optimization_barrier((tuple(values), others))[0]


def after(value, *others):
    return after_all((value,), *others)[0]


def whole(values):
    shape = values.shape
    return pl.BlockSpec(shape, lambda *_: (0,) * len(shape))


def call(body, outs, operands, in_specs=None, out_specs=None, grid=(1,), scalars=None, scratch=()):
    in_specs = [s or whole(v) for s, v in zip(in_specs or [None] * len(operands), operands)]
    out_specs = [s or whole(o) for s, o in zip(out_specs or [None] * len(outs), outs)]
    return pl.pallas_call(
        body,
        out_shape=outs,
        grid_spec=pltpu.PrefetchScalarGridSpec(
            num_scalar_prefetch=0 if scalars is None else 1,
            grid=grid,
            in_specs=in_specs,
            out_specs=out_specs,
            scratch_shapes=list(scratch),
        ),
        cost_estimate=pl.CostEstimate(flops=0, bytes_accessed=1024, transcendentals=0),
        compiler_params=pltpu.CompilerParams(vmem_limit_bytes=60 * 1024 * 1024),
    )(*([] if scalars is None else [scalars]), *operands)


def array(shape, kind):
    return jax.ShapeDtypeStruct(shape, kind)


def unit_rows(values):
    return values * lax.rsqrt(jnp.mean(values * values, axis=-1, keepdims=True) + EPS)


def project(tokens, gain, weights, headgate, cotangent, places, groups):
    rows, width = tokens.shape
    half = rows // 2
    sizes = [w.shape[0] // groups for w in weights]
    heads = headgate.shape[0]
    head_width = sizes[1]
    per_group = heads // groups
    middle = width // 2

    def body(at, x_ref, g_ref, q_ref, k_ref, v_ref, h_ref, c_ref, *refs):
        pieces, (normed_out, side_out, core_out, grad_out, gate_out, normed_s, gate_s) = (
            refs[:groups],
            refs[groups:],
        )
        step = pl.program_id(0)

        @pl.when(step == 0)
        def _():
            normed = (unit_rows(x_ref[...].astype(F32)) * g_ref[...].astype(F32)).astype(BF16)
            normed_s[...] = normed
            normed_out[...] = normed
            gate_s[...] = jax.nn.sigmoid(right_dot(normed, h_ref[...]))
            start = pl.multiple_of(at[groups] * half, half)
            grad_out[...] = c_ref[pl.ds(start, half), :]
            own = pl.multiple_of(at[groups + 1] * middle, middle)
            other = pl.multiple_of((1 - at[groups + 1]) * middle, middle)
            side_out[...] = normed_s[pl.ds(start, half), pl.ds(own, middle)]
            core_out[...] = normed_s[pl.ds(start, half), pl.ds(other, middle)]

        normed = normed_s[...]
        piece = jnp.concatenate(
            [right_dot(normed, w[...], BF16) for w in (q_ref, k_ref, v_ref)], axis=1
        )
        for place in range(groups):

            @pl.when(step == place)
            def _(place=place):
                pieces[place][...] = piece

        lane = lax.broadcasted_iota(jnp.int32, gate_s.shape, 1)
        for h in range(per_group):
            column = jnp.where(lane == at[step] * per_group + h, gate_s[...], 0.0)
            column = jnp.sum(column, axis=1, keepdims=True)
            gate_out[:, h * head_width : (h + 1) * head_width] = jnp.broadcast_to(
                column, (rows, head_width)
            )

    out = call(
        body,
        [array((rows, sum(sizes)), BF16)] * groups
        + [
            array((rows, width), BF16),
            array((half, middle), BF16),
            array((half, middle), BF16),
            array((half, width), BF16),
            array((groups * rows, per_group * head_width), F32),
        ],
        [tokens, gain, *weights, headgate, cotangent],
        [None, None]
        + [pl.BlockSpec((size, width), lambda k, at: (at[k], 0)) for size in sizes]
        + [None, None],
        [None] * (groups + 4)
        + [pl.BlockSpec((rows, per_group * head_width), lambda k, at: (k, 0))],
        grid=(groups,),
        scalars=places,
        scratch=[pltpu.VMEM((rows, width), BF16), pltpu.VMEM((rows, heads), F32)],
    )
    return (out[:groups], *out[groups:])


def turn(values, cosine, sine):
    return values * cosine + pltpu.roll(values, values.shape[-1] // 2, 1) * sine


def head_forward(pieces, cosine, sine, query_gain, key_gain):
    rows = pieces[0].shape[0]
    owned = rows * len(pieces)
    head_width = query_gain.shape[1]
    query_width = pieces[0].shape[1] - 2 * head_width

    def body(*refs):
        inputs = refs[: len(pieces)]
        cos_ref, sin_ref, qg_ref, kg_ref, q_out, kv_out = refs[len(pieces) :]
        for place, ref in enumerate(inputs):
            at = slice(place * rows, (place + 1) * rows)
            cos, sin = cos_ref[at, :], sin_ref[at, :]
            for first in range(0, query_width + head_width, head_width):
                gain = (qg_ref if first < query_width else kg_ref)[...]
                unit = unit_rows(ref[:, first : first + head_width].astype(F32)) * gain
                turned = turn(unit, cos, sin).astype(BF16)
                if first < query_width:
                    q_out[at, first : first + head_width] = turned
                else:
                    kv_out[at, :head_width] = turned
            kv_out[at, head_width:] = ref[:, query_width + head_width :]

    return call(
        body,
        [array((owned, query_width), BF16), array((owned, 2 * head_width), BF16)],
        [*pieces, cosine, sine, query_gain, key_gain],
    )


def head_backward(pieces, cosine, sine, query_gain, key_gain, grad_queries, pair_kept, pair_arrived):
    rows = pieces[0].shape[0]
    count = len(pieces)
    head_width = query_gain.shape[1]
    query_width = pieces[0].shape[1] - 2 * head_width

    def body(*refs):
        inputs = refs[:count]
        cos_ref, sin_ref, qg_ref, kg_ref, dq_ref, kept_ref, arrived_ref = refs[count : count + 7]
        outs, (stack_out, gains_out) = refs[count + 7 : 2 * count + 7], refs[2 * count + 7 :]
        gains = [jnp.zeros((1, head_width), F32) for _ in range(2)]
        for place, ref in enumerate(inputs):
            at = slice(place * rows, (place + 1) * rows)
            cos, sin = cos_ref[at, :], sin_ref[at, :]
            pair = kept_ref[at, :] + arrived_ref[at, :].astype(F32)
            for first in range(0, query_width + head_width, head_width):
                is_query = first < query_width
                gain = (qg_ref if is_query else kg_ref)[...]
                raw = ref[:, first : first + head_width].astype(F32)
                grad = dq_ref[at, first : first + head_width] if is_query else pair[:, :head_width]
                inverse = lax.rsqrt(jnp.mean(raw * raw, axis=-1, keepdims=True) + EPS)
                back, terms = normalize_back(raw, inverse, gain, turn(grad, cos, -sin))
                outs[place][:, first : first + head_width] = back.astype(BF16)
                which = 0 if is_query else 1
                gains[which] = gains[which] + jnp.sum(terms, axis=0, keepdims=True)
            outs[place][:, query_width + head_width :] = pair[:, head_width:].astype(BF16)
            stack_out[at, :] = outs[place][...]
        gains_out[0:1, :] = gains[0]
        gains_out[1:2, :] = gains[1]

    out = call(
        body,
        [array(pieces[0].shape, BF16)] * count
        + [array((count * rows, pieces[0].shape[1]), BF16), array((2, head_width), F32)],
        [*pieces, cosine, sine, query_gain, key_gain, grad_queries, pair_kept, pair_arrived],
    )
    return (out[:count], out[count], out[count + 1])


def stacked_heads(values, head_width):
    return jnp.concatenate(
        [values[:, h : h + head_width] for h in range(0, values.shape[1], head_width)], axis=0
    )


def unstacked_heads(values, rows):
    return jnp.concatenate(
        [values[h : h + rows] for h in range(0, values.shape[0], rows)], axis=1
    )


def key_chunk(total):
    return math.gcd(total, 512)


def chunk_loop(total, step):
    chunk = key_chunk(total)
    count = total // chunk
    if count <= 4:
        for index in range(count):
            step(index * chunk, chunk)
    else:
        pl.loop(0, count)(lambda index: step(pl.multiple_of(index * chunk, chunk), chunk))


def row_bounds(at, step, rows, items, blocks):
    row = at[items + step] + lax.broadcasted_iota(jnp.int32, (rows, 1), 0)
    begin = jnp.zeros((rows, 1), jnp.int32)
    for item in range(items):
        begin = jnp.maximum(begin, jnp.where(row >= at[item], at[item], 0))
    return (row, begin)


def masked_bias(key_ref, row, begin, start, chunk, copies):
    keys = key_ref[:, pl.ds(start, chunk)]
    bias = jnp.where((keys >= begin) & (keys <= row), 0.0, NEG)
    return jnp.concatenate([bias] * copies, axis=0)


def load_pairs(pairs, keys_s, values_s, head_width):
    start = 0
    for ref in pairs:
        rows = ref.shape[0]
        keys_s[start : start + rows, :] = ref[:, :head_width]
        values_s[start : start + rows, :] = ref[:, head_width:]
        start += rows


def attend(queries, pairs, key_index, bounds, blocks, score_scale):
    owned, query_width = queries.shape
    rows = owned // blocks
    head_width = pairs[0].shape[1] // 2
    copies = query_width // head_width
    total = key_index.shape[1]
    count = len(pairs)
    tall = rows * copies

    def body(at_rows, q_ref, *refs):
        pair_refs = refs[:count]
        key_ref, o_out, l_out = refs[count : count + 3]
        lows = refs[count + 3 : count + 3 + blocks]
        keys_s, values_s, scores_s, most_s, sum_s, acc_s = refs[count + 3 + blocks :]
        step = pl.program_id(0)
        row, begin = row_bounds(at_rows, step, rows, bounds.shape[0] - blocks, blocks)

        @pl.when(step == 0)
        def _():
            load_pairs(pair_refs, keys_s, values_s, head_width)

        query = stacked_heads(q_ref[...], head_width)
        most_s[...] = jnp.full(most_s.shape, NEG, F32)
        sum_s[...] = jnp.zeros(sum_s.shape, F32)
        acc_s[...] = jnp.zeros(acc_s.shape, F32)

        def first(start, chunk):
            at = pl.ds(start, chunk)
            scores = right_dot(query, keys_s[at, :]) * score_scale
            scores = scores + masked_bias(key_ref, row, begin, start, chunk, copies)
            scores_s[:, at] = scores
            most_s[...] = jnp.maximum(most_s[...], jnp.max(scores, axis=1, keepdims=True))

        def second(start, chunk):
            at = pl.ds(start, chunk)
            expo = jnp.exp(scores_s[:, at] - most_s[...])
            scores_s[:, at] = expo
            sum_s[...] += jnp.sum(expo, axis=1, keepdims=True)

        chunk_loop(total, first)
        chunk_loop(total, second)
        inverse = 1.0 / sum_s[...]

        def third(start, chunk):
            at = pl.ds(start, chunk)
            probs = (scores_s[:, at] * inverse).astype(BF16)
            acc_s[...] += plain_dot(probs, values_s[at, :])

        chunk_loop(total, third)
        attended = unstacked_heads(acc_s[...], rows)
        o_out[...] = attended
        log_sum = jnp.broadcast_to(most_s[...] + jnp.log(sum_s[...]), (tall, head_width))
        l_out[...] = unstacked_heads(log_sum, rows)
        for place in range(blocks):

            @pl.when(step == place)
            def _(place=place):
                lows[place][...] = attended.astype(BF16)

    def by_step(shape):
        return pl.BlockSpec(shape, lambda i, at: (i, 0))

    out = call(
        body,
        [array((owned, query_width), F32)] * 2 + [array((rows, query_width), BF16)] * blocks,
        [queries, *pairs, key_index],
        [by_step((rows, query_width))] + [None] * (count + 1),
        [by_step((rows, query_width))] * 2 + [None] * blocks,
        grid=(blocks,),
        scalars=bounds,
        scratch=[
            pltpu.VMEM((total, head_width), BF16),
            pltpu.VMEM((total, head_width), BF16),
            pltpu.VMEM((tall, total), F32),
            pltpu.VMEM((tall, 1), F32),
            pltpu.VMEM((tall, 1), F32),
            pltpu.VMEM((tall, head_width), F32),
        ],
    )
    return (out[0], out[1], out[2:])


def attend_back(queries, pairs, key_index, bounds, grads, attended, log_sums, score_scale):
    blocks = len(grads)
    owned, query_width = queries.shape
    rows = owned // blocks
    head_width = pairs[0].shape[1] // 2
    copies = query_width // head_width
    total = key_index.shape[1]
    count = len(pairs)
    tall = rows * copies
    half = total // 2

    def body(at_rows, q_ref, o_ref, l_ref, *refs):
        pair_refs, grad_refs = refs[:count], refs[count : count + blocks]
        key_ref, dq_out, kept_out, sent_out = refs[count + blocks : count + blocks + 4]
        keys_s, values_s, grads_s, dq_s, pair_s = refs[count + blocks + 4 :]
        step = pl.program_id(0)
        row, begin = row_bounds(at_rows, step, rows, bounds.shape[0] - blocks, blocks)

        @pl.when(step == 0)
        def _():
            load_pairs(pair_refs, keys_s, values_s, head_width)
            for place, ref in enumerate(grad_refs):
                grads_s[place] = ref[...]
            pair_s[...] = jnp.zeros(pair_s.shape, F32)

        query = stacked_heads(q_ref[...], head_width)
        grad = stacked_heads(grads_s[step], head_width)
        out = stacked_heads(o_ref[...], head_width)
        log_sum = stacked_heads(l_ref[...], head_width)[:, :1]
        delta = jnp.sum(grad.astype(F32) * out, axis=1, keepdims=True)
        dq_s[...] = jnp.zeros(dq_s.shape, F32)

        def each(start, chunk):
            at = pl.ds(start, chunk)
            keys, values = keys_s[at, :], values_s[at, :]
            scores = right_dot(query, keys) * score_scale
            scores = scores + masked_bias(key_ref, row, begin, start, chunk, copies)
            probs = jnp.exp(scores - log_sum)
            grad_scores = (probs * (right_dot(grad, values) - delta)).astype(BF16)
            dq_s[...] += plain_dot(grad_scores, keys)
            pair_s[at, :head_width] += outer_dot(grad_scores, query) * score_scale
            pair_s[at, head_width:] += outer_dot(probs.astype(BF16), grad)

        chunk_loop(total, each)
        dq_out[...] = unstacked_heads(dq_s[...], rows) * score_scale

        @pl.when(step == blocks - 1)
        def _():
            kept_out[...] = pair_s[:half, :]
            sent_out[...] = pair_s[half:, :].astype(BF16)

    def by_step(shape):
        return pl.BlockSpec(shape, lambda i, at: (i, 0))

    return call(
        body,
        [
            array((owned, query_width), F32),
            array((half, 2 * head_width), F32),
            array((half, 2 * head_width), BF16),
        ],
        [queries, attended, log_sums, *pairs, *grads, key_index],
        [by_step((rows, query_width))] * 3 + [None] * (count + blocks + 1),
        [by_step((rows, query_width)), None, None],
        grid=(blocks,),
        scalars=bounds,
        scratch=[
            pltpu.VMEM((total, head_width), BF16),
            pltpu.VMEM((total, head_width), BF16),
            pltpu.VMEM((blocks, rows, query_width), BF16),
            pltpu.VMEM((tall, head_width), F32),
            pltpu.VMEM((total, 2 * head_width), F32),
        ],
    )


def merge(attended, gate_value, merge_weight, tokens, places):
    groups = len(attended)
    rows, query_width = attended[0].shape
    width = tokens.shape[1]
    half = rows // 2

    def body(at, g_ref, w_ref, x_ref, *refs):
        inputs = refs[:groups]
        gated_out, sent_out, kept_out, stack_s, acc_s = refs[groups:]
        step = pl.program_id(0)

        @pl.when(step == 0)
        def _():
            for place, ref in enumerate(inputs):
                stack_s[place] = ref[...]
            acc_s[...] = jnp.zeros(acc_s.shape, F32)

        gated = (stack_s[step].astype(F32) * g_ref[...]).astype(BF16)
        gated_out[...] = gated
        acc_s[...] += right_dot(gated, w_ref[...])

        @pl.when(step == groups - 1)
        def _():
            own = pl.multiple_of(at[groups] * half, half)
            other = pl.multiple_of((1 - at[groups]) * half, half)
            sent_out[...] = acc_s[pl.ds(other, half), :].astype(BF16)
            kept_out[...] = acc_s[pl.ds(own, half), :] + x_ref[pl.ds(own, half), :].astype(F32)

    return call(
        body,
        [
            array((rows, groups * query_width), BF16),
            array((half, width), BF16),
            array((half, width), F32),
        ],
        [gate_value, merge_weight, tokens, *attended],
        [
            pl.BlockSpec((rows, query_width), lambda k, at: (k, 0)),
            pl.BlockSpec((width, query_width), lambda k, at: (0, at[k])),
            None,
        ]
        + [None] * groups,
        [pl.BlockSpec((rows, query_width), lambda k, at: (0, at[k])), None, None],
        grid=(groups,),
        scalars=places,
        scratch=[
            pltpu.VMEM((groups, rows, query_width), BF16),
            pltpu.VMEM((rows, width), F32),
        ],
    )


def second_norm(kept, arrived, gain):
    def body(kept_ref, arrived_ref, gain_ref, hidden_out, normed_out):
        hidden = kept_ref[...] + arrived_ref[...].astype(F32)
        hidden_out[...] = hidden
        normed_out[...] = (unit_rows(hidden) * gain_ref[...].astype(F32)).astype(BF16)

    return call(body, [array(kept.shape, F32), array(kept.shape, BF16)], [kept, arrived, gain])


def unit_copies(sources, which, target, semaphores):
    count = sources[0].shape[0] // 3
    return [
        pltpu.make_async_copy(
            source.at[pl.ds(which * count, count), :],
            target.at[pl.ds(place * count, count), :],
            semaphores.at[place],
        )
        for place, source in enumerate(sources)
    ]


def anywhere(values):
    return [pl.BlockSpec(memory_space=pl.ANY) for _ in values]


def fill_rows(pieces, target):
    start = 0
    for ref in pieces:
        target[start : start + ref.shape[0], :] = ref[...]
        start += ref.shape[0]


def act_gradient(pieces, stacks):
    rows, width = sum(piece.shape[0] for piece in pieces), pieces[0].shape[1]
    count, blocks = len(pieces), len(stacks)
    hidden = stacks[0].shape[0] // 3 * blocks
    half = hidden // 2

    def body(*refs):
        inputs, sources = refs[:count], refs[count : count + blocks]
        rows_out, grad_out, down_s, sems = refs[count + blocks :]
        copies = unit_copies(sources, 2, down_s, sems)
        for copy in copies:
            copy.start()
        fill_rows(inputs, rows_out)
        for h in range(2):
            for copy in copies[h * blocks // 2 : (h + 1) * blocks // 2]:
                copy.wait()
            grad_out[h] = right_dot(rows_out[...], down_s[h * half : (h + 1) * half, :])

    return call(
        body,
        [array((rows, width), BF16), array((2, rows, half), F32)],
        [*pieces, *stacks],
        [None] * count + anywhere(stacks),
        scratch=[pltpu.VMEM((hidden, width), BF16), pltpu.SemaphoreType.DMA((blocks,))],
    )


def feed(pieces, grad_act, stacks, part, kind):
    rows, width = sum(piece.shape[0] for piece in pieces), pieces[0].shape[1]
    count, blocks = len(pieces), len(stacks)
    hidden = stacks[0].shape[0] // 3 * blocks
    half = hidden // 2

    def body(*refs):
        inputs = refs[:count]
        grad_ref, sources = refs[count], refs[count + 1 : count + 1 + blocks]
        rows_out, left_out, sum_out, gate_s, up_s, sems = refs[count + 1 + blocks :]
        gate_copies = unit_copies(sources, 0, gate_s, sems.at[0])
        up_copies = unit_copies(sources, 1, up_s, sems.at[1])
        for pair in zip(gate_copies, up_copies):
            for copy in pair:
                copy.start()
        fill_rows(inputs, rows_out)
        for h in range(2):
            for place in range(h * blocks // 2, (h + 1) * blocks // 2):
                gate_copies[place].wait()
                up_copies[place].wait()
            at = slice(h * half, (h + 1) * half)
            gate_pre = right_dot(rows_out[...], gate_s[at, :])
            up_pre = right_dot(rows_out[...], up_s[at, :])
            sigma = jax.nn.sigmoid(gate_pre)
            grad = grad_ref[h]
            left_out[2, h] = (gate_pre * sigma * up_pre).astype(BF16)
            left_out[0, h] = (grad * up_pre * sigma * (1.0 + gate_pre * (1.0 - sigma))).astype(BF16)
            left_out[1, h] = (grad * gate_pre * sigma).astype(BF16)
        total = plain_dot(left_out[0, 0], gate_s[:half, :])
        total = total + plain_dot(left_out[0, 1], gate_s[half:, :])
        total = total + plain_dot(left_out[1, 0], up_s[:half, :])
        total = total + plain_dot(left_out[1, 1], up_s[half:, :])
        sum_out[...] = total.astype(kind)

    return call(
        body,
        [
            array((rows, width), BF16),
            array((3, 2, rows, half), BF16),
            array((rows, width), kind),
        ],
        [*pieces, grad_act, *stacks],
        [None] * count
        + [pl.BlockSpec((2, rows, half), lambda i: (0, part, 0))]
        + anywhere(stacks),
        scratch=[
            pltpu.VMEM((hidden, width), BF16),
            pltpu.VMEM((hidden, width), BF16),
            pltpu.SemaphoreType.DMA((2, blocks)),
        ],
    )


def branch(lefts, stacks):
    rows, half = lefts[0].shape[2:]
    width, blocks = stacks[0].shape[1], len(stacks)

    def body(near_ref, far_ref, *refs):
        kept_out, sent_out, down_s, sems = refs[blocks:]
        copies = unit_copies(refs[:blocks], 2, down_s, sems)
        for copy in copies:
            copy.start()
        for copy in copies:
            copy.wait()
        for act_ref, out in ((far_ref, sent_out), (near_ref, kept_out)):
            total = plain_dot(act_ref[0, 0], down_s[:half, :])
            total = total + plain_dot(act_ref[0, 1], down_s[half:, :])
            out[...] = total.astype(out.dtype)

    return call(
        body,
        [array((rows, width), F32), array((rows, width), BF16)],
        [*lefts, *stacks],
        [pl.BlockSpec((1, 2, rows, half), lambda i: (2, 0, 0, 0))] * 2 + anywhere(stacks),
        scratch=[pltpu.VMEM((2 * half, width), BF16), pltpu.SemaphoreType.DMA((blocks,))],
    )


def unit_gradients(lefts, inputs_low, grads_low):
    rows, half = lefts[0].shape[2:]
    width = grads_low.shape[1]

    def body(near_ref, far_ref, near_inputs, far_inputs, grads_ref, kept_out, sent_out):
        h, which = pl.program_id(0), pl.program_id(1)

        def put(near, far):
            value = outer_dot(near_ref[0, 0], near) + outer_dot(far_ref[0, 0], far)

            @pl.when(h == 0)
            def _():
                kept_out[...] = value

            @pl.when(h == 1)
            def _():
                sent_out[...] = value.astype(BF16)

        pl.when(which < 2)(lambda: put(near_inputs[...], far_inputs[...]))
        pl.when(which == 2)(lambda: put(grads_ref[:rows, :], grads_ref[rows:, :]))

    return call(
        body,
        [array((3 * half, width), F32), array((3 * half, width), BF16)],
        [*lefts, *inputs_low, grads_low],
        [pl.BlockSpec((1, 1, rows, half), lambda h, m: (m, h, 0, 0))] * 2 + [None] * 3,
        [
            pl.BlockSpec((half, width), lambda h, m: (jnp.where(h == 0, m, 2), 0)),
            pl.BlockSpec((half, width), lambda h, m: (jnp.where(h == 0, 0, m), 0)),
        ],
        grid=(2, 3),
    )


def add_units(kept, arrived):
    count, width = kept.shape[0] // 6, kept.shape[1]

    def body(kept_ref, arrived_ref, own_out, sent_out):
        own_out[...] = kept_ref[:count, :] + arrived_ref[:count, :].astype(F32)
        sent_out[...] = (kept_ref[count:, :] + arrived_ref[count:, :].astype(F32)).astype(BF16)

    return call(
        body,
        [array((3 * count, width), F32), array((3 * count, width), BF16)],
        [kept, arrived],
        [pl.BlockSpec((2 * count, width), lambda i: (i, 0))] * 2,
        [pl.BlockSpec((count, width), lambda i: (i, 0))] * 2,
        grid=(3,),
    )


def add_split(kept, arrived, parts):
    rows = kept.shape[0] // parts

    def body(kept_ref, arrived_ref, *outs):
        for place, out in enumerate(outs):
            at = slice(place * rows, (place + 1) * rows)
            out[...] = (kept_ref[at, :] + arrived_ref[at, :].astype(F32)).astype(out.dtype)

    shape = (rows, kept.shape[1])
    out = call(
        body, [array(shape, F32)] + [array(shape, BF16)] * (parts - 1), [kept, arrived]
    )
    return (out[0], out[1:])


def hidden_gradient(kept, arrived, hidden, gain, grad_half):
    rows, width = kept.shape

    def body(kept_ref, hidden_ref, gain_ref, grad_ref, *refs):
        low_out, terms_out = refs[-2:]
        upstream = kept_ref[...]
        for ref in refs[:-2]:
            upstream = upstream + ref[...].astype(F32)
        values = hidden_ref[...]
        inverse = lax.rsqrt(jnp.mean(values * values, axis=-1, keepdims=True) + EPS)
        back, terms = normalize_back(values, inverse, gain_ref[...].astype(F32), upstream)
        low_out[...] = (grad_ref[...].astype(F32) + back).astype(BF16)
        terms_out[...] = jnp.sum(terms, axis=0, keepdims=True)

    return call(
        body,
        [array((rows, width), BF16), array((1, width), F32)],
        [kept, hidden, gain, grad_half, *arrived],
    )


def merge_back(own, other, merge_weight, gate_value, attended, places, head_width):
    groups = len(attended)
    half, width = own.shape
    rows = 2 * half
    query_width = attended[0].shape[1]
    per_group = query_width // head_width
    heads = groups * per_group
    middle = width // 2

    def body(at, own_ref, other_ref, w_ref, g_ref, *refs):
        inputs = refs[:groups]
        pieces = refs[groups : 2 * groups]
        hidden_out, core_out, logit_out, stack_s, logit_s = refs[2 * groups :]
        step = pl.program_id(0)

        @pl.when(step == 0)
        def _():
            for place, ref in enumerate(inputs):
                stack_s[place] = ref[...]
            hidden_out[pl.ds(pl.multiple_of(at[groups] * half, half), half), :] = own_ref[...]
            hidden_out[pl.ds(pl.multiple_of((1 - at[groups]) * half, half), half), :] = other_ref[
                ...
            ]
            away = pl.multiple_of((1 - at[groups + 1]) * middle, middle)
            core_out[...] = hidden_out[:, pl.ds(away, middle)]
            logit_s[...] = jnp.zeros(logit_s.shape, F32)

        grad = plain_dot(hidden_out[...], w_ref[...])
        gate = g_ref[...]
        low = (grad * gate).astype(BF16)
        for place in range(groups):

            @pl.when(step == place)
            def _(place=place):
                pieces[place][...] = low

        terms = grad * stack_s[step].astype(F32)
        slope = gate * (1.0 - gate)
        lane = lax.broadcasted_iota(jnp.int32, (rows, heads), 1)
        for h in range(per_group):
            at_head = slice(h * head_width, (h + 1) * head_width)
            column = jnp.sum(terms[:, at_head], axis=1, keepdims=True)
            column = column * slope[:, h * head_width : h * head_width + 1]
            logit_s[...] += jnp.where(lane == at[step] * per_group + h, column, 0.0)

        @pl.when(step == groups - 1)
        def _():
            logit_out[...] = logit_s[...].astype(BF16)

    out = call(
        body,
        [array((rows, query_width), BF16)] * groups
        + [
            array((rows, width), BF16),
            array((rows, middle), BF16),
            array((rows, heads), BF16),
        ],
        [own, other, merge_weight, gate_value, *attended],
        [
            None,
            None,
            pl.BlockSpec((width, query_width), lambda k, at: (0, at[k])),
            pl.BlockSpec((rows, query_width), lambda k, at: (k, 0)),
        ]
        + [None] * groups,
        grid=(groups,),
        scalars=places,
        scratch=[
            pltpu.VMEM((groups, rows, query_width), BF16),
            pltpu.VMEM((rows, heads), F32),
        ],
    )
    return (out[:groups], *out[groups:])


def merge_gradient(hidden_low, hidden_core, gated, gated_core, places, groups):
    rows, width = hidden_low.shape
    wide = gated.shape[1]
    part = width // 4

    def body(at, own_ref, core_ref, gated_ref, gated_core_ref, kept_out, *sent_outs):
        away, piece = 1 - at[groups + 2], part // 2
        for place, begin, size, out in (
            (away, 0, piece, sent_outs[0]),
            (away, piece, piece, sent_outs[1]),
            (at[groups + 2], 0, part, kept_out),
        ):
            first = pl.multiple_of((2 * at[groups + 1] + place) * part + begin, size)
            second = pl.multiple_of(place * part + begin, size)
            value = outer_dot(own_ref[:, pl.ds(first, size)], gated_ref[...])
            value = value + outer_dot(core_ref[:, pl.ds(second, size)], gated_core_ref[...])
            out[...] = value.astype(out.dtype)

    return call(
        body,
        [array((part, wide), F32)] + [array((part // 2, wide), BF16)] * 2,
        [hidden_low, hidden_core, gated, gated_core],
        scalars=places,
    )


def add_split_at(kept, arrived, places):
    parts = places.shape[0]
    rows = kept.shape[0] // parts
    count = len(arrived)

    def body(at, kept_ref, *refs):
        outs, arrived_s = refs[count:-1], refs[-1]
        fill_rows(refs[:count], arrived_s)
        for place, out in enumerate(outs):
            rows_at = pl.ds(pl.multiple_of(at[place] * rows, rows), rows)
            out[...] = (kept_ref[rows_at, :] + arrived_s[rows_at, :].astype(F32)).astype(out.dtype)

    shape = (rows, kept.shape[1])
    out = call(
        body,
        [array(shape, F32)] + [array(shape, BF16)] * (parts - 1),
        [kept, *arrived],
        scalars=places,
        scratch=[pltpu.VMEM(kept.shape, BF16)],
    )
    return (out[0], out[1:])


def input_part(pieces, logits, weights, headgate, places):
    groups = len(pieces)
    rows = pieces[0].shape[0]
    width = headgate.shape[1]
    sizes = [w.shape[0] // groups for w in weights]

    def body(at, q_ref, k_ref, v_ref, h_ref, l_ref, *refs):
        inputs = refs[:groups]
        part_out, stack_s, acc_s = refs[groups:]
        step = pl.program_id(0)

        @pl.when(step == 0)
        def _():
            for place, ref in enumerate(inputs):
                stack_s[place] = ref[...]
            acc_s[...] = plain_dot(l_ref[...], h_ref[...])

        values = stack_s[step]
        total, first = acc_s[...], 0
        for size, ref in zip(sizes, (q_ref, k_ref, v_ref)):
            total = total + plain_dot(values[:, first : first + size], ref[...])
            first += size
        acc_s[...] = total

        @pl.when(step == groups - 1)
        def _():
            part_out[...] = acc_s[...].astype(BF16)

    return call(
        body,
        [array((rows, width), BF16)],
        [*weights, headgate, logits, *pieces],
        [pl.BlockSpec((size, width), lambda k, at: (at[k], 0)) for size in sizes]
        + [None] * (2 + groups),
        grid=(groups,),
        scalars=places,
        scratch=[pltpu.VMEM((groups, rows, sum(sizes)), BF16), pltpu.VMEM((rows, width), F32)],
    )[0]


def input_gradient(part, arrived, tokens, gain, hidden_low):
    rows, width = tokens.shape

    def body(part_ref, arrived_ref, x_ref, gain_ref, hidden_ref, grad_out, terms_out):
        upstream = part_ref[...].astype(F32) + arrived_ref[...].astype(F32)
        values = x_ref[...].astype(F32)
        inverse = lax.rsqrt(jnp.mean(values * values, axis=-1, keepdims=True) + EPS)
        back, terms = normalize_back(values, inverse, gain_ref[...].astype(F32), upstream)
        grad_out[...] = hidden_ref[...].astype(F32) + back
        terms_out[...] = jnp.sum(terms, axis=0, keepdims=True)

    return call(
        body,
        [array((rows, width), F32), array((1, width), F32)],
        [part, arrived, tokens, gain, hidden_low],
    )


def head_gradient(pieces, core_pieces, own_rows, other_rows, places, groups):
    count = len(pieces)
    rows, wide = pieces[0].shape
    half = rows // 2
    middle = other_rows.shape[1]
    part = middle // 2

    def body(at, *refs):
        inputs, core_ref, own_refs = refs[:count], refs[count], refs[count + 1 : 2 * count + 1]
        other_ref, kept_out, sent_out, left_s, right_s = refs[2 * count + 1 :]
        start = 0
        for which in (at[groups], 1 - at[groups]):
            for place, ref in enumerate(inputs):
                own = pl.multiple_of(which * half, half)
                core = pl.multiple_of(which * half + place * rows, half)
                left_s[start : start + half, :] = ref[pl.ds(own, half), :]
                left_s[start + half : start + rows, :] = core_ref[pl.ds(core, half), :]
                start += rows
        fill_rows([*own_refs, other_ref], right_s)
        left = left_s[...]
        for place, out in ((1 - at[groups + 2], sent_out), (at[groups + 2], kept_out)):
            columns = pl.ds(pl.multiple_of(place * part, part), part)
            out[...] = outer_dot(left, right_s[:, columns], out.dtype)

    return call(
        body,
        [array((wide, part), F32), array((wide, part), BF16)],
        [*pieces, core_pieces, *own_rows, other_rows],
        scalars=places,
        scratch=[
            pltpu.VMEM((2 * count * rows, wide), BF16),
            pltpu.VMEM((2 * count * rows, middle), BF16),
        ],
    )


def add_columns_at(kept, arrived, places):
    rows, width = kept.shape
    middle = width // 2

    def body(at, kept_ref, arrived_ref, kept_out, sent_out):
        for place, out in enumerate((kept_out, sent_out)):
            columns = pl.ds(pl.multiple_of(at[place] * middle, middle), middle)
            out[...] = (kept_ref[:, columns] + arrived_ref[:, columns].astype(F32)).astype(
                out.dtype
            )

    return call(
        body,
        [array((rows, middle), F32), array((rows, middle), BF16)],
        [kept, arrived],
        scalars=places,
    )


def assemble(parts, order, heights, row_blocks, column_blocks, before=()):
    count = order.shape[0] // 2
    wide = parts[0].shape[1]
    tall = sum(heights)
    rows = sum(part.shape[0] for part in parts)
    assert rows == count * tall
    begins = [sum(heights[:i]) for i in range(len(heights))]

    def body(at, *refs):
        inputs = refs[: len(parts)]
        outs = refs[len(parts) + len(before) : len(parts) + len(before) + len(heights)]
        values_s, sems = refs[-2:]
        copies, start = [], 0
        for ref in inputs:
            for first in range(0, ref.shape[0], tall):
                block = start // tall
                values_s[start : start + tall, :] = ref[first : first + tall, :].astype(F32)
                for which, (height, begin, out) in enumerate(zip(heights, begins, outs)):
                    row = pl.multiple_of(at[block] * height, height)
                    column = pl.multiple_of(at[count + block] * wide, wide)
                    copy = pltpu.make_async_copy(
                        values_s.at[pl.ds(start + begin, height), :],
                        out.at[pl.ds(row, height), pl.ds(column, wide)],
                        sems.at[block, which],
                    )
                    copy.start()
                    copies.append(copy)
                start += tall
        for copy in copies:
            copy.wait()

    return pl.pallas_call(
        body,
        out_shape=[
            array((height * row_blocks, wide * column_blocks), F32) for height in heights
        ],
        grid_spec=pltpu.PrefetchScalarGridSpec(
            num_scalar_prefetch=1,
            grid=(1,),
            in_specs=[whole(part) for part in parts] + anywhere(before),
            out_specs=anywhere(heights),
            scratch_shapes=[
                pltpu.VMEM((rows, wide), F32),
                pltpu.SemaphoreType.DMA((count, len(heights))),
            ],
        ),
        input_output_aliases={1 + len(parts) + i: i for i in range(len(before))},
        cost_estimate=pl.CostEstimate(flops=0, bytes_accessed=1024, transcendentals=0),
        compiler_params=pltpu.CompilerParams(vmem_limit_bytes=60 * 1024 * 1024),
    )(order, *parts, *before)


def shards(
    tokens,
    item_lengths,
    first_gain,
    query_weight,
    key_weight,
    value_weight,
    headgate_weight,
    merge_weight,
    query_norm,
    key_norm,
    second_gain,
    gate_weight,
    up_weight,
    down_weight,
    out_cotangent,
):
    sp_size = lax.axis_size("sp")
    device = lax.axis_index("sp")
    side = lax.axis_index("tp")
    local_rows, width = tokens.shape
    half_rows = local_rows // 2
    head_width = query_norm.shape[0]
    local_heads = query_weight.shape[0] // head_width
    groups = key_weight.shape[0] // head_width
    query_width = local_heads // groups * head_width
    score_scale = 1.0 / math.sqrt(head_width)

    bits = sp_size.bit_length() - 1
    group_step = 1 << (bits // 2)
    group_masks = [group_step * k for k in range(1, groups)]
    all_group_masks = [0] + group_masks
    group_bits = group_step * (groups - 1)
    rest = [1 << b for b in range(1, bits) if not (1 << b) & group_bits] + [1]
    rest_count = 1 << len(rest)
    rest_masks = [
        sum(mask for b, mask in enumerate(rest) if r >> b & 1) for r in range(rest_count)
    ]
    row_masks = rest[:-1]
    order = [outer ^ mask for outer in rest_masks for mask in all_group_masks]
    own_group = (device // group_step) % groups
    own_rest = sum(((device // mask) % 2) * (1 << b) for b, mask in enumerate(rest))
    group_places = own_group ^ jnp.arange(groups, dtype=jnp.int32)
    rest_places = own_rest ^ jnp.arange(rest_count, dtype=jnp.int32)
    rest_bits = [(own_rest >> b) & 1 for b in range(len(rest))]
    places = jnp.concatenate(
        [group_places, jnp.stack([side, rest_bits[-1], rest_bits[-2]]).astype(jnp.int32)]
    )

    def level(b):
        return jnp.stack([rest_bits[b], 1 - rest_bits[b]]).astype(jnp.int32)

    device_order = device ^ jnp.array(order, dtype=jnp.int32)

    def across_groups(pieces):
        return [pieces[0]] + [exchange(p, mask) for p, mask in zip(pieces[1:], group_masks)]

    def row_groups(values):
        return [values] + [exchange(values, mask) for mask in group_masks]

    def row_pieces(pieces, *others):
        pieces = list(pieces)
        for mask in row_masks:
            pieces.append(exchange(after(stack_rows(*pieces), *others), mask))
        return pieces

    def add_rows(kept, arrived):
        for mask in reversed(row_masks[:-1]):
            kept, (sent,) = add_split(kept, arrived, 2)
            arrived = exchange(sent, mask)
        return add_split(kept, arrived, groups)

    first_gain_row = first_gain.reshape(1, width)
    second_gain_row = second_gain.reshape(1, width)
    query_gain = query_norm.astype(F32).reshape(1, head_width)
    key_gain = key_norm.astype(F32).reshape(1, head_width)

    projections = (query_weight, key_weight, value_weight)
    sent, normed_low, normed_half, normed_core, grad_half, gate_value = project(
        tokens,
        first_gain_row,
        projections,
        headgate_weight,
        out_cotangent,
        places,
        groups,
    )
    raw = across_groups(sent)
    own_stack = after(stack_rows(gate_weight, up_weight, down_weight), *sent)
    side_stack = swap(own_stack)
    core_stack = exchange(own_stack, 1)
    raw = after_all(raw, core_stack)

    item = jnp.arange(item_lengths.shape[0], dtype=jnp.int32)
    item_starts = jnp.sum(
        jnp.where(item[:, None] < item[None, :], item_lengths[:, None], 0), axis=0
    )
    within = jnp.arange(local_rows, dtype=jnp.int32)
    row_devices = device ^ jnp.array(all_group_masks, dtype=jnp.int32)
    row_index = (row_devices[:, None] * local_rows + within[None, :]).reshape(-1, 1)
    key_index = (device_order[:, None] * local_rows + within[None, :]).reshape(1, -1)
    begins = jnp.max(
        jnp.where(item_starts[None, :] <= row_index, item_starts[None, :], 0),
        axis=1,
        keepdims=True,
    )
    lane = jnp.arange(head_width, dtype=jnp.int32)
    frequency = THETA ** (
        -2.0 * (lane % (head_width // 2)).astype(F32) / head_width
    )
    angles = (row_index - begins).astype(F32) * frequency[None, :]
    cosine = jnp.cos(angles)
    sine = jnp.sin(angles) * jnp.where(lane < head_width // 2, -1.0, 1.0)

    bounds = jnp.concatenate([item_starts, row_devices * local_rows]).astype(jnp.int32)
    queries, pair_own = head_forward(raw, cosine, sine, query_gain, key_gain)
    grad_groups = row_groups(after(grad_half, pair_own))
    pairs = [pair_own]
    for mask in rest:
        pairs.append(exchange(pairs[0] if len(pairs) == 1 else stack_rows(*pairs), mask))
    attended, log_sums, attended_low = attend(
        queries, pairs, key_index, bounds, groups, score_scale
    )
    attended_rows = across_groups(after_all(attended_low, *grad_groups))
    attended_rows = after_all(attended_rows, side_stack)
    side_core_stack = exchange(after(side_stack, *attended_rows), 1)
    gated_low, sent, kept = merge(attended_rows, gate_value, merge_weight, tokens, places)
    normed_side = stack_rows(normed_half, exchange(after(normed_core, *attended_rows), 1))
    arrived = after(swap(sent), side_core_stack, normed_side)
    gated_core = exchange(gated_low, 1)
    hidden, second_low = second_norm(kept, arrived, second_gain_row)

    stacks = [own_stack, side_stack, core_stack, side_core_stack]
    second_groups = row_groups(second_low)
    grads_low, grad_act = act_gradient(row_pieces(grad_groups, *attended_low), stacks)
    inputs = row_pieces(second_groups, grads_low, gated_core)
    side_rows = row_groups(after(normed_side, *second_groups))
    near = feed(inputs[:-1], grad_act, stacks, 0, F32)
    far_inputs = after_all(inputs[-1:], near[2], *side_rows)
    far = feed(far_inputs, grad_act, stacks, 1, BF16)
    (near_low, near_left, kept), (far_low, far_left, sent) = near, far
    lefts = [near_left, far_left]
    arrived = exchange(sent, row_masks[-1])
    other_rows = swap(after(stack_rows(*side_rows), sent))
    branch_kept, branch_sent = branch(lefts, stacks)
    unit_kept, unit_sent = unit_gradients(lefts, [near_low, far_low], grads_low)
    kept, sent = add_rows(after(kept, branch_sent, unit_sent, other_rows), arrived)
    branch_arrived = exchange(after(branch_sent, kept), row_masks[-1])
    unit_arrived = exchange(after(unit_sent, kept), 1)
    arrived = [exchange(piece, mask) for piece, mask in zip(sent, group_masks)]
    unit_own, unit_sent = add_units(unit_kept, unit_arrived)
    hidden_half, second_terms = hidden_gradient(
        after(kept, unit_own), arrived, hidden, second_gain_row, grad_half
    )
    branch_kept, branch_sent = add_rows(branch_kept, branch_arrived)
    branch_first = exchange(branch_sent[0], group_masks[0])
    hidden_other = after(swap(hidden_half), *branch_sent)
    grad_pieces, hidden_low, hidden_core, grad_logit_low = merge_back(
        hidden_half, hidden_other, merge_weight, gate_value, attended_rows, places, head_width
    )

    grad_grouped = across_groups(after_all(grad_pieces, branch_first))
    merge_kept, *merge_sent = merge_gradient(
        hidden_low, exchange(hidden_core, 1), gated_low, gated_core, places, groups
    )
    merge_first = exchange(merge_sent[0], rest[-2])

    grad_grouped = after_all(grad_grouped, merge_kept)
    branch_second = exchange(after(branch_sent[1], *grad_grouped), group_masks[1])
    grad_queries, kept, sent = attend_back(
        queries,
        pairs,
        key_index,
        bounds,
        grad_grouped,
        attended,
        log_sums,
        score_scale,
    )
    sent = after(sent, branch_second, merge_first)
    for mask in reversed(rest[1:]):
        kept, (sent,) = add_split(kept, exchange(sent, mask), 2)
    branch_third = [
        exchange(after(piece, branch_second), mask)
        for piece, mask in zip(branch_sent[2:], group_masks[2:])
    ]
    branch_arrived = [branch_first, branch_second, *branch_third]
    arrived = exchange(sent, rest[0])
    merge_second = exchange(after(merge_sent[1], arrived), rest[-2])
    head_grads, head_stack, head_gains = head_backward(
        raw, cosine, sine, query_gain, key_gain, grad_queries, kept, arrived
    )
    head_core = exchange(head_stack, 1)

    back = across_groups(after_all(head_grads, *branch_arrived, head_core))
    part = input_part(back, grad_logit_low, projections, headgate_weight, places)
    part_other = swap(part)
    input_grad, first_terms = input_gradient(
        part, part_other, tokens, first_gain_row, hidden_low
    )
    kept, sent = head_gradient(head_grads, head_core, side_rows, other_rows, places, groups)
    arrived = exchange(after(sent, merge_second), rest[-2])
    for b in reversed(range(len(rest) - 2)):
        kept, sent = add_columns_at(kept, arrived, level(b))
        arrived = exchange(sent, rest[b])
    head_block = (kept + arrived.astype(F32)).astype(BF16)
    merge_arrived = [merge_first, merge_second]
    for b in reversed(range(len(rest) - 2)):
        merge_kept, (merge_sent,) = add_split_at(merge_kept, merge_arrived, level(b))
        merge_arrived = [exchange(merge_sent, rest[b])]

    merge_kept, merge_sent = add_split_at(merge_kept, merge_arrived, group_places)
    merge_sent = after_all(merge_sent, *back)
    merge_arrived = [exchange(piece, mask) for piece, mask in zip(merge_sent, group_masks)]
    unit_side = swap(after(unit_sent, part_other))
    query_block, key_block, value_block = (
        head_block[:query_width],
        head_block[query_width : query_width + head_width],
        head_block[query_width + head_width :],
    )

    def all_parts(pieces, *others):
        parts = [stack_rows(*pieces)]
        for mask in row_masks:
            parts = parts + [exchange(after(part, *others), mask) for part in parts]
        return parts

    def core_parts(parts, *others):
        return [exchange(after(part, *others), 1) for part in parts]

    query_groups = row_groups(after(query_block, *merge_arrived))
    merge_block = merge_kept
    for piece in merge_arrived:
        merge_block = merge_block + piece.astype(F32)
    merge_groups = row_groups(after(merge_block.astype(BF16), *query_groups))
    query_parts = all_parts(query_groups)
    key_groups = row_groups(after(key_block, unit_side, *merge_groups, *query_parts))
    merge_parts = all_parts(merge_groups)
    query_core = core_parts(query_parts, *merge_groups)
    value_groups = row_groups(after(value_block, *key_groups, *merge_parts, *query_core))
    key_parts = all_parts(key_groups)
    merge_core = core_parts(merge_parts, *key_groups)
    value_parts = all_parts(after_all(value_groups, *key_parts, *merge_core))
    key_core = core_parts(key_parts)

    block_rows = jnp.tile(group_places, rest_count)
    block_columns = jnp.repeat(rest_places, groups)
    strips = block_columns * groups + block_rows
    block_order = jnp.concatenate([block_rows, block_columns])
    (query_grad,) = assemble(
        [*query_parts, *query_core], block_order, (query_width,), groups, rest_count
    )
    (merge_grad,) = assemble(
        [*merge_parts, *merge_core],
        jnp.concatenate([strips, jnp.zeros_like(strips)]),
        (width // sp_size,),
        sp_size,
        1,
    )
    (key_grad,) = assemble(
        [*key_parts, *key_core], block_order, (head_width,), groups, rest_count
    )
    value_core = core_parts(value_parts, query_grad, merge_grad, key_grad)
    (value_grad,) = assemble(
        [*value_parts, *value_core], block_order, (head_width,), groups, rest_count
    )

    for piece in branch_arrived:
        branch_kept = branch_kept + piece.astype(F32)
    output_half = (hidden + branch_kept).astype(BF16)
    output_other = swap(output_half)
    layer_output = jnp.where(
        side == 0,
        stack_rows(output_half, output_other),
        stack_rows(output_other, output_half),
    )
    unit_sum = unit_own + unit_side.astype(F32)
    units = gate_weight.shape[0]
    gate_acc, up_acc, down_acc = (unit_sum[i * units : (i + 1) * units] for i in range(3))

    headgate_part = outer_dot(grad_logit_low, normed_low)
    gains = jnp.concatenate(
        [head_gains[0], head_gains[1], jnp.zeros((width - 2 * head_width,), F32)]
    )
    sides = stack_rows(second_terms, gains[None])
    sides = sides + swap(sides)
    small = after(stack_rows(headgate_part, first_terms, sides), *merge_arrived)
    for mask in rest:
        small = small + exchange(small, mask)
    small = after(small, *value_groups)
    small = small + sum(exchange(small, mask) for mask in group_masks)

    return (
        layer_output,
        input_grad,
        small[local_heads],
        query_grad,
        key_grad,
        value_grad,
        small[:local_heads],
        merge_grad,
        small[local_heads + 2, :head_width],
        small[local_heads + 2, head_width : 2 * head_width],
        small[local_heads + 1],
        gate_acc,
        up_acc,
        down_acc,
    )


def solution(mesh):
    return jax.shard_map(
        shards,
        mesh=mesh,
        in_specs=(
            P("sp", None),
            P(),
            P(),
            P("tp", None),
            P("tp", None),
            P("tp", None),
            P("tp", None),
            P(None, "tp"),
            P(),
            P(),
            P(),
            P(("tp", "sp"), None),
            P(("tp", "sp"), None),
            P(("tp", "sp"), None),
            P("sp", None),
        ),
        out_specs=(
            P("sp", None),
            P("sp", None),
            P(),
            P("tp", None),
            P("tp", None),
            P("tp", None),
            P("tp", None),
            P(None, "tp"),
            P(),
            P(),
            P(),
            P(("tp", "sp"), None),
            P(("tp", "sp"), None),
            P(("tp", "sp"), None),
        ),
        check_vma=False,
    )
```

time: 587 us -> 477 us (0.81)
  Pallas kernels: 0 us -> 163 us
  other arithmetic: 91.3 us -> 19 us
  waiting for transfers between devices: 226 us -> 163 us
  matrix products: 58.5 us -> 0.23 us
  local copies, waits for them, and re-layouts: 90 us -> 33.3 us
  starting transfers between devices: 108 us -> 87.1 us
    pallas_call x0 -> x27, Pallas kernels: none -> 163 us  [the longest x23 142 us: call(): pl.pallas_call(body, out_shape=outs, grid_spec=pltpu.PrefetchScalarGridSp...]
    ppermute x62 -> x77, waiting for transfers between devices: 201 us -> 153 us  [exchange(): return lax.ppermute(values, 'sp', [(i, i ^ mask) for i in range(size)])]
    dot_general x21 -> x0, matrix products: 39.6 us -> none  [the longest x8 16.5 us: right_dot(): lax.dot_general(first_matrix, second_matrix, (((1,), (1,)), ((), ())), pr...]
    unnamed x221 -> x179, local copies, waits for them, and re-layouts: 42.3 us -> 23.4 us
    ppermute x62 -> x77, starting transfers between devices: 99.1 us -> 81.2 us  [exchange(): return lax.ppermute(values, 'sp', [(i, i ^ mask) for i in range(size)])]
    convert_element_type x16 -> x4, other arithmetic: 18 us -> 1.55 us  [the longest x1 1.18 us: shards(): merge_groups = row_groups(after(merge_block.astype(BF16), *query_groups))]
    ppermute x12 -> x8, waiting for transfers between devices: 24.7 us -> 10.8 us  [swap(): return lax.ppermute(values, 'tp', [(0, 1), (1, 0)])]
    add x17 -> x7, other arithmetic: 17.5 us -> 3.84 us  [the longest x1 3.03 us: shards(): unit_sum = unit_own + unit_side.astype(F32)]
  transfers between devices with their start and end apart: 74 -> 85, of which waited for: 30 -> 40; matrix products, arithmetic and copies ran while one was open for 37% -> 7% of each run, Pallas kernels for 0% -> 27%
where the time goes in v2:
time: 477 us; the launch traced here: 468 us
  Pallas kernels  163 us (34%)
  waiting for transfers between devices  163 us (34%)
  starting transfers between devices  87.1 us (18%)
  local copies, waits for them, and re-layouts  33.3 us (7%)
  other arithmetic  19 us (4%)
    ppermute x77, waiting for transfers between devices, exchange(): return lax.ppermute(values, 'sp', [(i, i ^ mask) for i in range(size)])  153 us
    pallas_call x23, Pallas kernels, call(): pl.pallas_call(body, out_shape=outs, grid_spec=pltpu.PrefetchScalarGridSp...  142 us
    ppermute x77, starting transfers between devices, exchange(): return lax.ppermute(values, 'sp', [(i, i ^ mask) for i in range(size)])  81.2 us
    unnamed x179, local copies, waits for them, and re-layouts  23.4 us
    pallas_call x4, Pallas kernels, assemble(): pl.pallas_call(body, out_shape=[array((height * row_blocks, wide * column...  21.2 us
    ppermute x8, waiting for transfers between devices, swap(): return lax.ppermute(values, 'tp', [(0, 1), (1, 0)])  10.8 us
  transfers between devices with their start and end apart: 85, of which 40 were waited for; matrix products, arithmetic and copies ran while one was open for 7% of the time, Pallas kernels for 27%

profile of v2, /device:TPU:17, one launch (start us, length us, event | category | flops | bytes accessed | tf_op | source)
XLA Modules:
  0.0 468.0 jit_solution(5331151630271340835)
XLA Ops:
  4.6 8.8 %shard_map.272 = (bf16[128,512]{1,0:T(8,128)(2,1)}, bf16[128,512]{1,0:T(8,128)(2,1)}, bf16[128,512]{1,0:T(8,128)(2,1)}, bf16[128,512]{1,0:T(8,128)(2,1)}, bf16[1...) custom-call(s32[7]{0:T(128)} %pad_add_fusion.at, ...), custom_call_target="tpu_custom_call" | custom-call | bytes 1024 | tf_op jit(solution)/shard_map/pallas_call | solution.py:139
  22.2 6.7 %collective-permute-done.2.refs_3_ = bf16[128,512]{1,0:T(8,128)(2,1)S(1)} collective-permute-done((bf16[128,512]{1,0:T(8,128)(2,1)}, bf16[128,512]{1,0:T(8,128)(2,1)S(1)}, u32[]{:S(2)}, u32[]{:S(2)}) %collective-permute-start.2) | collective-permute-done | bytes 131104 | tf_op jit(solution)/shard_map/ppermute | solution.py:73
  48.6 9.5 %shard_map.274 = (f32[512,256]{1,0:T(8,128)}, f32[512,256]{1,0:T(8,128)}, bf16[128,256]{1,0:T(8,128)(2,1)}, bf16[128,256]{1,0:T(8,128)(2,1)}, bf16[128,256]{1,0:T(8,128)(2,1)}, /*index=5*/bf16[128,256]{1,0:T(8,128)(2,1)}) custom-call(s32[8]{0:T(128)} %pad_add_fusion.1.at_rows, bf16[512,256]{1,0:T(8,128)(2,1)} %get-tuple-element.163.q_ref, ...), custom_call_target="tpu_custom_call" | custom-call | bytes 1024 | tf_op jit(solution)/shard_map/pallas_call | solution.py:139
  80.4 6.4 %shard_map.275 = (bf16[128,1024]{1,0:T(8,128)(2,1)}, bf16[64,2048]{1,0:T(8,128)(2,1)}, f32[64,2048]{1,0:T(8,128)}) custom-call(s32[7]{0:T(128)} %pad_add_fusion.at, f32[512,256]{1,0:T(8,128)} %get-tuple-element.153.g_ref, bf16[2048,1024]{1,0:T(8,128)(2,1)} %w_ref.3, bf16[128,2048]{1,0:T(8,128)(2,1)} %x_ref.5, bf16[128,256]{1,0:T(8,128)(2,1)} %get-tuple-element.175.refs_0_, ...), custom_call_target="tpu_custom_call" | custom-call | bytes 1024 | tf_op jit(solution)/shard_map/pallas_call | solution.py:139
  104.0 6.7 %shard_map.277 = (bf16[512,2048]{1,0:T(8,128)(2,1)}, f32[2,512,384]{2,1,0:T(8,128)}) custom-call(bf16[64,2048]{1,0:T(8,128)(2,1)} %get-tuple-element.170.refs_0_.grad_ref, bf16[64,2048]{1,0:T(8,128)(2,1)} %collective-permute-done.6.refs_1_, bf16[64,2048]{1,0:T(8,128)(2,1)} %collective-permute-done.7.refs_2_, bf16[64,2048]{1,0:T(8,128)(2,1)} %copy-done.15, ...), custom_call_target="tpu_custom_call" | custom-call | bytes 1024 | tf_op jit(solution)/shard_map/pallas_call | solution.py:139
  126.7 9.6 %shard_map.278 = (bf16[256,2048]{1,0:T(8,128)(2,1)}, bf16[3,2,256,384]{3,2,1,0:T(8,128)(2,1)}, f32[256,2048]{1,0:T(8,128)}) custom-call(bf16[64,2048]{1,0:T(8,128)(2,1)} %get-tuple-element.187.refs_0_, bf16[64,2048]{1,0:T(8,128)(2,1)} %collective-permute-done.16.refs_1_, bf16[64,2048]{1,0:T(8,128)(2,1)} %collective-permute-done.17.refs_2_, ...), custom_call_target="tpu_custom_call" | custom-call | bytes 1024 | tf_op jit(solution)/shard_map/pallas_call | solution.py:139
  136.3 6.9 %collective-permute-done.23.refs_7_ = bf16[128,1024]{1,0:T(8,128)(2,1)S(1)} collective-permute-done((bf16[128,1024]{1,0:T(8,128)(2,1)S(1)}, bf16[128,1024]{1,0:T(8,128)(2,1)S(1)}, u32[]{:S(2)}, u32[]{:S(2)}) %collective-permute-start.23) | collective-permute-done | bytes 262176 | tf_op jit(solution)/shard_map/ppermute | solution.py:73
  145.2 9.2 %shard_map.279 = (bf16[256,2048]{1,0:T(8,128)(2,1)}, bf16[3,2,256,384]{3,2,1,0:T(8,128)(2,1)}, bf16[256,2048]{1,0:T(8,128)(2,1)}) custom-call(bf16[256,2048]{1,0:T(8,128)(2,1)} %copy-done.11, f32[2,512,384]{2,1,0:T(8,128)} %get-tuple-element.189.refs_4_.refs_1_, bf16[576,2048]{1,0:T(8,128)(2,1)} %copy-done, ...), custom_call_target="tpu_custom_call" | custom-call | bytes 1024 | tf_op jit(solution)/shard_map/pallas_call | solution.py:139
  157.1 13.1 %shard_map.281 = (f32[1152,2048]{1,0:T(8,128)}, bf16[1152,2048]{1,0:T(8,128)(2,1)}) custom-call(bf16[3,2,256,384]{3,2,1,0:T(8,128)(2,1)} %get-tuple-element.190.near_ref, bf16[3,2,256,384]{3,2,1,0:T(8,128)(2,1)} %get-tuple-element.197.far_ref, bf16[256,2048]{1,0:T(8,128)(2,1)} %get-tuple-element.200.near_inputs, ...), custom_call_target="tpu_custom_call" | custom-call | bytes 1024 | tf_op jit(solution)/shard_map/pallas_call | solution.py:139
  170.1 6.7 %shard_map.280 = (f32[256,2048]{1,0:T(8,128)}, bf16[256,2048]{1,0:T(8,128)(2,1)}) custom-call(bf16[3,2,256,384]{3,2,1,0:T(8,128)(2,1)} %get-tuple-element.190.near_ref, bf16[3,2,256,384]{3,2,1,0:T(8,128)(2,1)} %get-tuple-element.197.far_ref, bf16[576,2048]{1,0:T(8,128)(2,1)} %copy-done, bf16[576,2048]{1,0:T(8,128)(2,1)} %collective-permute-done.12.refs_6_.refs_3_.refs_1_, ...), custom_call_target="tpu_custom_call" | custom-call | bytes 1024 | tf_op jit(solution)/shard_map/pallas_call | solution.py:139
  193.4 8.6 %shard_map.284 = (f32[576,2048]{1,0:T(8,128)}, bf16[576,2048]{1,0:T(8,128)(2,1)}) custom-call(f32[1152,2048]{1,0:T(8,128)} %get-tuple-element.211.kept_ref, bf16[1152,2048]{1,0:T(8,128)(2,1)} %collective-permute-done.29.arrived_ref), custom_call_target="tpu_custom_call" | custom-call | bytes 1024 | tf_op jit(solution)/shard_map/pallas_call | solution.py:139
  202.2 12.0 %collective-permute-done.32.refs_2_ = bf16[64,2048]{1,0:T(8,128)(2,1)S(1)} collective-permute-done((bf16[64,2048]{1,0:T(8,128)(2,1)}, bf16[64,2048]{1,0:T(8,128)(2,1)S(1)}, u32[]{:S(2)}, u32[]{:S(2)}) %collective-permute-start.32) | collective-permute-done | bytes 262176 | tf_op jit(solution)/shard_map/ppermute | solution.py:73
  225.1 6.4 %shard_map.286 = (bf16[128,256]{1,0:T(8,128)(2,1)}, bf16[128,256]{1,0:T(8,128)(2,1)}, bf16[128,256]{1,0:T(8,128)(2,1)}, bf16[128,256]{1,0:T(8,128)(2,1)}, bf16[1...) custom-call(s32[7]{0:T(128)} %pad_add_fusion.at, ...), custom_call_target="tpu_custom_call" | custom-call | bytes 1024 | tf_op jit(solution)/shard_map/pallas_call | solution.py:139
  251.0 12.4 %shard_map.288 = (f32[512,256]{1,0:T(8,128)}, f32[1024,256]{1,0:T(8,128)}, bf16[1024,256]{1,0:T(8,128)(2,1)}) custom-call(s32[8]{0:T(128)} %pad_add_fusion.1.at_rows, bf16[512,256]{1,0:T(8,128)(2,1)} %get-tuple-element.163.q_ref, f32[512,256]{1,0:T(8,128)} %get-tuple-element.239.o_ref, f32[512,256]{1,0:T(8,128)} %get-tuple-element.240.l_ref, ...), custom_call_target="tpu_custom_call" | custom-call | bytes 1024 | tf_op jit(solution)/shard_map/pallas_call | solution.py:139
  270.9 7.5 %collective-permute-done.43.refs_10_ = bf16[512,256]{1,0:T(8,128)(2,1)S(1)} collective-permute-done((bf16[512,256]{1,0:T(8,128)(2,1)}, bf16[512,256]{1,0:T(8,128)(2,1)S(1)}, u32[]{:S(2)}, u32[]{:S(2)}) %collective-permute-start.43) | collective-permute-done | bytes 262176 | tf_op jit(solution)/shard_map/ppermute | solution.py:73
  292.0 6.0 %collective-permute-done.50.refs_1_ = bf16[256,1024]{1,0:T(8,128)(2,1)S(1)} collective-permute-done((bf16[256,1024]{1,0:T(8,128)(2,1)S(1)}, bf16[256,1024]{1,0:T(8,128)(2,1)S(1)}, u32[]{:S(2)}, u32[]{:S(2)}) %collective-permute-start.50) | collective-permute-done | bytes 524320 | tf_op jit(solution)/shard_map/ppermute | solution.py:73
  305.6 6.6 %collective-permute-done.47.refs_3_ = bf16[128,512]{1,0:T(8,128)(2,1)S(1)} collective-permute-done((bf16[128,512]{1,0:T(8,128)(2,1)S(1)}, bf16[128,512]{1,0:T(8,128)(2,1)S(1)}, u32[]{:S(2)}, u32[]{:S(2)}) %collective-permute-start.47) | collective-permute-done | bytes 131104 | tf_op jit(solution)/shard_map/ppermute | solution.py:73
  314.9 7.2 %shard_map.291.part_ref = bf16[128,2048]{1,0:T(8,128)(2,1)} custom-call(s32[7]{0:T(128)} %pad_add_fusion.at, bf16[1024,2048]{1,0:T(8,128)(2,1)} %q_ref.3, bf16[512,2048]{1,0:T(8,128)(2,1)} %k_ref.3, bf16[512,2048]{1,0:T(8,128)(2,1)} %v_ref.3, bf16[8,2048]{1,0:T(8,128)(2,1)} %h_ref.3, bf16[128,8]{1,0:T(8,128)(2,1)} %get-tuple-element.238.l_ref, ...), custom_call_target="tpu_custom_call" | custom-call | bytes 1024 | tf_op jit(solution)/shard_map/pallas_call | solution.py:139
  325.1 11.3 %collective-permute-done.53 = bf16[128,1024]{1,0:T(8,128)(2,1)S(1)} collective-permute-done((bf16[128,1024]{1,0:T(8,128)(2,1)}, bf16[128,1024]{1,0:T(8,128)(2,1)S(1)}, u32[]{:S(2)}, u32[]{:S(2)}) %collective-permute-start.53) | collective-permute-done | bytes 262176 | tf_op jit(solution)/shard_map/ppermute | solution.py:73
  348.7 11.5 %collective-permute-done.60 = bf16[256,512]{1,0:T(8,128)(2,1)S(1)} collective-permute-done((bf16[256,512]{1,0:T(8,128)(2,1)S(1)}, bf16[256,512]{1,0:T(8,128)(2,1)S(1)}, u32[]{:S(2)}, u32[]{:S(2)}) %collective-permute-start.60) | collective-permute-done | bytes 262176 | tf_op jit(solution)/shard_map/ppermute | solution.py:73
  371.0 12.6 %collective-permute-done.63 = bf16[128,1024]{1,0:T(8,128)(2,1)S(1)} collective-permute-done((bf16[128,1024]{1,0:T(8,128)(2,1)S(1)}, bf16[128,1024]{1,0:T(8,128)(2,1)S(1)}, u32[]{:S(2)}, u32[]{:S(2)}) %collective-permute-start.63) | collective-permute-done | bytes 262176 | tf_op jit(solution)/shard_map/ppermute | solution.py:73
  405.5 6.3 %shard_map.295 = f32[1024,2048]{1,0:T(8,128)} custom-call(s32[32]{0:T(128)} %pad_add_fusion.2.at, bf16[1024,512]{1,0:T(8,128)(2,1)} %constant_dynamic-update-slice_fusion.2.refs_0_, bf16[1024,512]{1,0:T(8,128)(2,1)} %collective-permute-done.64.refs_1_, bf16[1024,512]{1,0:T(8,128)(2,1)} %collective-permute-done.69.refs_2_, ...), custom_call_target="tpu_custom_call" | custom-call | bytes 1024 | tf_op jit(solution)/shard_map/pallas_call | solution.py:1055
  430.0 7.8 %collective-permute-done.77.refs_1_ = bf16[512,512]{1,0:T(8,128)(2,1)} collective-permute-done((bf16[512,512]{1,0:T(8,128)(2,1)S(1)}, bf16[512,512]{1,0:T(8,128)(2,1)}, u32[]{:S(2)}, u32[]{:S(2)}) %collective-permute-start.77) | collective-permute-done | bytes 524320 | tf_op jit(solution)/shard_map/ppermute | solution.py:73
  445.4 6.3 %shard_map.297 = f32[2048,1024]{1,0:T(8,128)} custom-call(s32[32]{0:T(128)} %concatenate.75.at, bf16[512,1024]{1,0:T(8,128)(2,1)} %constant_dynamic-update-slice_fusion.6.refs_0_, bf16[512,1024]{1,0:T(8,128)(2,1)} %collective-permute-done.68.refs_1_, bf16[512,1024]{1,0:T(8,128)(2,1)} %copy-done.8, bf16[512,1024]{1,0:T(8,128)(2,1)} %copy-done.9), custom_call_target="tpu_custom_call" | custom-call | bytes 1024 | tf_op jit(solution)/shard_map/pallas_call | solution.py:1055
  (406 shorter events, 260.2 us)
Async XLA Ops:
  16.9 53.6 %collective-permute-start.12 = (bf16[576,2048]{1,0:T(8,128)(2,1)S(1)}, bf16[576,2048]{1,0:T(8,128)(2,1)}, u32[]{:S(2)}, u32[]{:S(2)}) collective-permute-start(bf16[576,2048]{1,0:T(8,128)(2,1)S(1)} %pad_maximum_fusion.refs_5_.refs_2_.refs_0_), channel_id=1, source_target_pairs={{0,16},{16,0},{1,17},{17,1},{2,18},{18,2},{3,19},{19,3},{4,20},{20... | collective-permute-start | bytes 7077896 | tf_op jit(solution)/shard_map/ppermute | solution.py:77
  44.1 22.0 %collective-permute-start.7 = (bf16[64,2048]{1,0:T(8,128)(2,1)S(1)}, bf16[64,2048]{1,0:T(8,128)(2,1)}, u32[]{:S(2)}, u32[]{:S(2)}) collective-permute-start(bf16[64,2048]{1,0:T(8,128)(2,1)S(1)} %copy-done.4), channel_id=1, source_target_pairs={{0,8},{1,9},{2,10},{3,11},{4,12},{5,13},{6,14},{7,15},{8,0},{9,1},... | collective-permute-start | bytes 786440 | tf_op jit(solution)/shard_map/ppermute | solution.py:73
  44.3 21.7 %collective-permute-start.6 = (bf16[64,2048]{1,0:T(8,128)(2,1)S(1)}, bf16[64,2048]{1,0:T(8,128)(2,1)}, u32[]{:S(2)}, u32[]{:S(2)}) collective-permute-start(bf16[64,2048]{1,0:T(8,128)(2,1)S(1)} %copy-done.4), channel_id=1, source_target_pairs={{0,4},{1,5},{2,6},{3,7},{4,0},{5,1},{6,2},{7,3},{8,12},{9,13},{10,... | collective-permute-start | bytes 786440 | tf_op jit(solution)/shard_map/ppermute | solution.py:73
  79.1 24.9 %collective-permute-start.19 = (bf16[256,2048]{1,0:T(8,128)(2,1)S(1)}, bf16[256,2048]{1,0:T(8,128)(2,1)}, u32[]{:S(2)}, u32[]{:S(2)}) collective-permute-start(bf16[256,2048]{1,0:T(8,128)(2,1)S(1)} %pad_maximum_fusion.1), channel_id=1, source_target_pairs={{0,2},{1,3},{2,0},{3,1},{4,6},{5,7},{6,4},{7,5},{8,10},{9,11},{10,... | collective-permute-start | bytes 3145736 | tf_op jit(solution)/shard_map/ppermute | solution.py:73
  98.2 21.7 %collective-permute-start.17 = (bf16[64,2048]{1,0:T(8,128)(2,1)}, bf16[64,2048]{1,0:T(8,128)(2,1)}, u32[]{:S(2)}, u32[]{:S(2)}) collective-permute-start(bf16[64,2048]{1,0:T(8,128)(2,1)} %get-tuple-element.187.refs_0_), channel_id=1, source_target_pairs={{0,8},{1,9},{2,10},{3,11},{4,12},{5,13},{6,14},{7,15},{8,0},{9,1},... | collective-permute-start | bytes 786440 | tf_op jit(solution)/shard_map/ppermute | solution.py:73
  100.4 19.6 %collective-permute-start.16 = (bf16[64,2048]{1,0:T(8,128)(2,1)}, bf16[64,2048]{1,0:T(8,128)(2,1)}, u32[]{:S(2)}, u32[]{:S(2)}) collective-permute-start(bf16[64,2048]{1,0:T(8,128)(2,1)} %get-tuple-element.187.refs_0_), channel_id=1, source_target_pairs={{0,4},{1,5},{2,6},{3,7},{4,0},{5,1},{6,2},{7,3},{8,12},{9,13},{10,... | collective-permute-start | bytes 786440 | tf_op jit(solution)/shard_map/ppermute | solution.py:73
  100.4 20.8 %collective-permute-start.20 = (bf16[128,1024]{1,0:T(8,128)(2,1)}, bf16[128,1024]{1,0:T(8,128)(2,1)}, u32[]{:S(2)}, u32[]{:S(2)}) collective-permute-start(bf16[128,1024]{1,0:T(8,128)(2,1)} %get-tuple-element.192.gated_ref), channel_id=1, source_target_pairs={{0,1},{1,0},{2,3},{3,2},{4,5},{5,4},{6,7},{7,6},{8,9},{9,8},{10,11... | collective-permute-start | bytes 786440 | tf_op jit(solution)/shard_map/ppermute | solution.py:73
  121.2 23.1 %collective-permute-start.21 = (bf16[256,2048]{1,0:T(8,128)(2,1)S(1)}, bf16[256,2048]{1,0:T(8,128)(2,1)S(1)}, u32[]{:S(2)}, u32[]{:S(2)}) collective-permute-start(bf16[256,2048]{1,0:T(8,128)(2,1)S(1)} %pad_maximum_fusion.2), channel_id=1, source_target_pairs={{0,2},{1,3},{2,0},{3,1},{4,6},{5,7},{6,4},{7,5},{8,10},{9,11},{10,... | collective-permute-start | bytes 3145736 | tf_op jit(solution)/shard_map/ppermute | solution.py:73
  122.7 20.4 %collective-permute-start.23 = (bf16[128,1024]{1,0:T(8,128)(2,1)S(1)}, bf16[128,1024]{1,0:T(8,128)(2,1)S(1)}, u32[]{:S(2)}, u32[]{:S(2)}) collective-permute-start(bf16[128,1024]{1,0:T(8,128)(2,1)S(1)} %constant_dynamic-update-slice_fusion.refs_5_), channel_id=1, source_target_pairs={{0,8},{1,9},{2,10},{3,11},{4,12},{5,13},{6,14},{7,15},{8,0},{9,1},... | collective-permute-start | bytes 786440 | tf_op jit(solution)/shard_map/ppermute | solution.py:73
  154.5 22.3 %collective-permute-start.25 = (bf16[512,1024]{1,0:T(8,128)(2,1)S(1)}, bf16[512,1024]{1,0:T(8,128)(2,1)S(1)}, u32[]{:S(2)}, u32[]{:S(2)}) collective-permute-start(bf16[512,1024]{1,0:T(8,128)(2,1)S(1)} %pad_maximum_fusion.3), channel_id=1, source_target_pairs={{0,16},{16,0},{1,17},{17,1},{2,18},{18,2},{3,19},{19,3},{4,20},{20... | collective-permute-start | bytes 3145736 | tf_op jit(solution)/shard_map/ppermute | solution.py:77
  155.8 21.7 %collective-permute-start.26 = (bf16[256,2048]{1,0:T(8,128)(2,1)}, bf16[256,2048]{1,0:T(8,128)(2,1)S(1)}, u32[]{:S(2)}, u32[]{:S(2)}) collective-permute-start(bf16[256,2048]{1,0:T(8,128)(2,1)} %get-tuple-element.203), channel_id=1, source_target_pairs={{0,2},{1,3},{2,0},{3,1},{4,6},{5,7},{6,4},{7,5},{8,10},{9,11},{10,... | collective-permute-start | bytes 3145736 | tf_op jit(solution)/shard_map/ppermute | solution.py:73
  185.5 32.3 %collective-permute-start.27 = (bf16[256,2048]{1,0:T(8,128)(2,1)S(1)}, bf16[256,2048]{1,0:T(8,128)(2,1)S(1)}, u32[]{:S(2)}, u32[]{:S(2)}) collective-permute-start(bf16[256,2048]{1,0:T(8,128)(2,1)S(1)} %copy-done.77), channel_id=1, source_target_pairs={{0,2},{1,3},{2,0},{3,1},{4,6},{5,7},{6,4},{7,5},{8,10},{9,11},{10,... | collective-permute-start | bytes 3145736 | tf_op jit(solution)/shard_map/ppermute | solution.py:73
  189.9 24.2 %collective-permute-start.32 = (bf16[64,2048]{1,0:T(8,128)(2,1)}, bf16[64,2048]{1,0:T(8,128)(2,1)S(1)}, u32[]{:S(2)}, u32[]{:S(2)}) collective-permute-start(bf16[64,2048]{1,0:T(8,128)(2,1)} %get-tuple-element.217), channel_id=1, source_target_pairs={{0,12},{1,13},{2,14},{3,15},{4,8},{5,9},{6,10},{7,11},{8,4},{9,5},... | collective-permute-start | bytes 786440 | tf_op jit(solution)/shard_map/ppermute | solution.py:73
  240.3 23.2 %collective-permute-start.41 = (bf16[256,1024]{1,0:T(8,128)(2,1)}, bf16[256,1024]{1,0:T(8,128)(2,1)S(1)}, u32[]{:S(2)}, u32[]{:S(2)}) collective-permute-start(bf16[256,1024]{1,0:T(8,128)(2,1)} %get-tuple-element.244), channel_id=1, source_target_pairs={{0,2},{1,3},{2,0},{3,1},{4,6},{5,7},{6,4},{7,5},{8,10},{9,11},{10,... | collective-permute-start | bytes 1572872 | tf_op jit(solution)/shard_map/ppermute | solution.py:73
  298.0 24.5 %collective-permute-start.56 = (bf16[512,512]{1,0:T(8,128)(2,1)}, bf16[512,512]{1,0:T(8,128)(2,1)S(1)}, u32[]{:S(2)}, u32[]{:S(2)}) collective-permute-start(bf16[512,512]{1,0:T(8,128)(2,1)} %get-tuple-element.273), channel_id=1, source_target_pairs={{0,2},{1,3},{2,0},{3,1},{4,6},{5,7},{6,4},{7,5},{8,10},{9,11},{10,... | collective-permute-start | bytes 1572872 | tf_op jit(solution)/shard_map/ppermute | solution.py:73
  314.6 21.8 %collective-permute-start.53 = (bf16[128,1024]{1,0:T(8,128)(2,1)}, bf16[128,1024]{1,0:T(8,128)(2,1)S(1)}, u32[]{:S(2)}, u32[]{:S(2)}) collective-permute-start(bf16[128,1024]{1,0:T(8,128)(2,1)} %get-tuple-element.269), channel_id=1, source_target_pairs={{0,12},{1,13},{2,14},{3,15},{4,8},{5,9},{6,10},{7,11},{8,4},{9,5},... | collective-permute-start | bytes 786440 | tf_op jit(solution)/shard_map/ppermute | solution.py:73
  338.9 23.2 %collective-permute-start.49 = (f32[2,2048]{1,0:T(2,128)S(1)}, f32[2,2048]{1,0:T(2,128)S(1)}, u32[]{:S(2)}, u32[]{:S(2)}) collective-permute-start(f32[2,2048]{1,0:T(2,128)S(1)} %pad_maximum_fusion.6), channel_id=1, source_target_pairs={{0,16},{16,0},{1,17},{17,1},{2,18},{18,2},{3,19},{19,3},{4,20},{20... | collective-permute-start | bytes 49160 | tf_op jit(solution)/shard_map/ppermute | solution.py:77
  339.1 21.1 %collective-permute-start.60 = (bf16[256,512]{1,0:T(8,128)(2,1)S(1)}, bf16[256,512]{1,0:T(8,128)(2,1)S(1)}, u32[]{:S(2)}, u32[]{:S(2)}) collective-permute-start(bf16[256,512]{1,0:T(8,128)(2,1)S(1)} %slice.54), channel_id=1, source_target_pairs={{0,12},{1,13},{2,14},{3,15},{4,8},{5,9},{6,10},{7,11},{8,4},{9,5},... | collective-permute-start | bytes 786440 | tf_op jit(solution)/shard_map/ppermute | solution.py:73
  341.0 51.8 %collective-permute-start.57 = (bf16[576,2048]{1,0:T(8,128)(2,1)}, bf16[576,2048]{1,0:T(8,128)(2,1)S(1)}, u32[]{:S(2)}, u32[]{:S(2)}) collective-permute-start(bf16[576,2048]{1,0:T(8,128)(2,1)} %get-tuple-element.275), channel_id=1, source_target_pairs={{0,16},{16,0},{1,17},{17,1},{2,18},{18,2},{3,19},{19,3},{4,20},{20... | collective-permute-start | bytes 7077896 | tf_op jit(solution)/shard_map/ppermute | solution.py:77
  360.9 29.9 %collective-permute-start.64 = (bf16[1024,512]{1,0:T(8,128)(2,1)}, bf16[1024,512]{1,0:T(8,128)(2,1)}, u32[]{:S(2)}, u32[]{:S(2)}) collective-permute-start(bf16[1024,512]{1,0:T(8,128)(2,1)} %constant_dynamic-update-slice_fusion.2.refs_0_), channel_id=1, source_target_pairs={{0,2},{1,3},{2,0},{3,1},{4,6},{5,7},{6,4},{7,5},{8,10},{9,11},{10,... | collective-permute-start | bytes 3145736 | tf_op jit(solution)/shard_map/ppermute | solution.py:73
  367.8 20.0 %collective-permute-start.62 = (bf16[128,1024]{1,0:T(8,128)(2,1)S(1)}, bf16[128,1024]{1,0:T(8,128)(2,1)S(1)}, u32[]{:S(2)}, u32[]{:S(2)}) collective-permute-start(bf16[128,1024]{1,0:T(8,128)(2,1)S(1)} %add_convert_fusion.1), channel_id=1, source_target_pairs={{0,8},{1,9},{2,10},{3,11},{4,12},{5,13},{6,14},{7,15},{8,0},{9,1},... | collective-permute-start | bytes 786440 | tf_op jit(solution)/shard_map/ppermute | solution.py:73
  367.8 20.0 %collective-permute-start.61 = (bf16[128,1024]{1,0:T(8,128)(2,1)S(1)}, bf16[128,1024]{1,0:T(8,128)(2,1)S(1)}, u32[]{:S(2)}, u32[]{:S(2)}) collective-permute-start(bf16[128,1024]{1,0:T(8,128)(2,1)S(1)} %add_convert_fusion.1), channel_id=1, source_target_pairs={{0,4},{1,5},{2,6},{3,7},{4,0},{5,1},{6,2},{7,3},{8,12},{9,13},{10,... | collective-permute-start | bytes 786440 | tf_op jit(solution)/shard_map/ppermute | solution.py:73
  390.6 25.1 %collective-permute-start.68 = (bf16[512,1024]{1,0:T(8,128)(2,1)}, bf16[512,1024]{1,0:T(8,128)(2,1)}, u32[]{:S(2)}, u32[]{:S(2)}) collective-permute-start(bf16[512,1024]{1,0:T(8,128)(2,1)} %constant_dynamic-update-slice_fusion.6.refs_0_), channel_id=1, source_target_pairs={{0,2},{1,3},{2,0},{3,1},{4,6},{5,7},{6,4},{7,5},{8,10},{9,11},{10,... | collective-permute-start | bytes 3145736 | tf_op jit(solution)/shard_map/ppermute | solution.py:73
  428.9 22.8 %collective-permute-start.78 = (bf16[512,512]{1,0:T(8,128)(2,1)S(1)}, bf16[512,512]{1,0:T(8,128)(2,1)S(1)}, u32[]{:S(2)}, u32[]{:S(2)}) collective-permute-start(bf16[512,512]{1,0:T(8,128)(2,1)S(1)} %constant_dynamic-update-slice_fusion.10.refs_0_), channel_id=1, source_target_pairs={{0,1},{1,0},{2,3},{3,2},{4,5},{5,4},{6,7},{7,6},{8,9},{9,8},{10,11... | collective-permute-start | bytes 1572872 | tf_op jit(solution)/shard_map/ppermute | solution.py:73
  (144 other events, 1592.2 us)
